TPU v7x, 32 devices: a whole 2x2x4 slice. The times are simulated.
32 devices in a mesh: blk: 8 (over z, x), head: 4 (over y, core).
Axes of the slice: x: 2, y: 2, z: 4, core: 2. Of those that a mesh axis runs over, the one named last changes fastest.
Arguments:
- ctx_q: bfloat16 [8192, 4096], P('blk', 'head'), may hold values from -120 to 120, as said below
- ctx_k: bfloat16 [8192, 1024], P('blk', 'head'), may hold values from -6 to 6
- ctx_v: bfloat16 [8192, 1024], P('blk', 'head'), may hold values from -6 to 6
- query_q: bfloat16 [8, 256, 4096], P('blk', None, 'head'), may hold values from -120 to 120, as said below
- query_k: bfloat16 [8, 256, 1024], P('blk', None, 'head'), may hold values from -6 to 6
- query_v: bfloat16 [8, 256, 1024], P('blk', None, 'head'), may hold values from -6 to 6
- out_weight: bfloat16 [4096, 4096], P('head', 'blk'), may hold values from -0.09375 to 0.09375
- anchor_index: int32 [1], replicated, may hold values from 0 to 7
- owner_index: int32 [1], replicated, may hold values from 0 to 7
- counts: int32 [8], replicated, may hold values from 256 to 1024, as said below
Outputs:
- ctx_out: bfloat16 [8192, 4096], P('blk', 'head')
- answer: bfloat16 [256, 4096], P(None, 'blk')
Inputs may be any that keep to these rules, and one draw needn't show every extreme that they name: `ctx_q`: row 5 mod 64 of a block or query slab may be a large multiple of a key row of the same head nearby. `query_q`: row 5 mod 64 of a slab may be a large multiple of a key row of the same head nearby. `counts`: some block has exactly 1024 valid tokens.
All inputs are finite; a program needn't handle non-finite values.
Results may differ from a plain program's by a relative error of at most 0.0056.
Values may be sent and summed in bfloat16 or wider, within the bound.
No kernel may reach another device: no remote copies, remote signals or barrier semaphores. Data moves between devices by JAX's collectives and lax.ppermute only.
A program may use at most 128 MiB of HBM per device.

v0:
```python
import functools
import math

import jax
import jax.numpy as jnp
from jax import lax
from jax.experimental import pallas as pl
from jax.experimental.pallas import tpu as pltpu
from jax.sharding import PartitionSpec as P


HEADS = 32
KV_HEADS = 8
GROUP = HEADS // KV_HEADS
HD = 128
C = HD**-0.5 * math.log2(math.e)
NEG = -1e30
NT = (((1,), (1,)), ((), ()))
TM = 256
VMEM = 14 << 20
WIDE = 61 << 20


def code_of(i):
    u = i >> 1
    return (i & 1) | ((u ^ (u >> 1)) << 1)


def decode_table(n):
    return {code_of(i): i for i in range(n)}


def log2_of(n):
    k = n.bit_length() - 1
    assert 1 << k == n
    return k


class Grid:
    def __init__(self, n_blk, n_head):
        self.n_blk, self.n_head = n_blk, n_head
        self.dims = log2_of(n_blk)

    def order(self, head):
        dims = list(range(self.dims))
        return dims if head & 1 == 0 else dims[1:] + dims[:1]

    def bit(self, step, odd):
        return jnp.where(odd, self.order(1)[step], self.order(0)[step])

    def hop(self, value, steps):
        back = decode_table(self.n_blk)
        pairs = []
        for i in range(self.n_blk):
            for h in range(self.n_head):
                j = back[code_of(i) ^ (1 << self.order(h)[steps])]
                pairs.append((i * self.n_head + h, j * self.n_head + h))
        return lax.ppermute(value, ("blk", "head"), pairs)

    def head_hop(self, value, bit):
        return lax.ppermute(value, "head", [(i, i ^ (1 << bit)) for i in range(self.n_head)])


def scores(q, k):
    return lax.dot_general(q, k, NT, preferred_element_type=jnp.float32)


def lane_max(s):
    m = s[:, :128]
    for j in range(1, s.shape[1] // 128):
        m = jnp.maximum(m, s[:, j * 128 : (j + 1) * 128])
    return jnp.max(m, axis=1, keepdims=True)


def weigh(p, v):
    wide = jnp.concatenate([v, jnp.ones_like(v)], axis=1)
    both = jnp.dot(p.astype(jnp.bfloat16), wide, preferred_element_type=jnp.float32)
    return both


def attend(s_parts, v_parts):
    m = functools.reduce(jnp.maximum, [lane_max(s) for s in s_parts])
    mc = m * C
    acc = None
    for s, v in zip(s_parts, v_parts):
        both = weigh(jnp.exp2(s * C - mc), v)
        acc = both if acc is None else acc + both
    return m, acc[:, HD:], acc[:, :HD]


def causal(n, width, first_col):
    r = lax.broadcasted_iota(jnp.int32, (n, width), 0)
    c = lax.broadcasted_iota(jnp.int32, (n, width), 1) + first_col
    return c <= r


def own_kernel(q_ref, k_ref, v_ref, o_ref, stat_ref):
    rows = q_ref.shape[0]
    h = pl.program_id(0)
    lane = lax.broadcasted_iota(jnp.int32, (TM, 128), 1)
    for i in range(rows // TM):
        at = pl.ds(i * TM, TM)
        q = q_ref[at, :]
        n = i * TM
        s_parts = [jnp.where(causal(TM, TM, 0), scores(q, k_ref[at, :]), NEG)]
        v_parts = [v_ref[at, :]]
        if n:
            s_parts.append(scores(q, k_ref[:n, :]))
            v_parts.append(v_ref[:n, :])
        m, total, o = attend(s_parts, v_parts)
        o_ref[at, :] = o
        stat = jnp.where(lane == h, m, stat_ref[at, :])
        stat_ref[at, :] = jnp.where(lane == h + 64, total, stat)


def own_call(q, k, v, lo, hi):
    rows = q.shape[0]
    n = hi - lo
    f32 = jnp.float32
    return pl.pallas_call(
        own_kernel,
        grid=(n,),
        in_specs=[
            pl.BlockSpec((rows, HD), lambda h: (0, lo + h)),
            pl.BlockSpec((rows, HD), lambda h: (0, (lo + h) // GROUP)),
            pl.BlockSpec((rows, HD), lambda h: (0, (lo + h) // GROUP)),
        ],
        out_specs=[
            pl.BlockSpec((rows, HD), lambda h: (0, h)),
            pl.BlockSpec((rows, 128), lambda h: (0, 0)),
        ],
        out_shape=[
            jax.ShapeDtypeStruct((rows, n * HD), f32),
            jax.ShapeDtypeStruct((rows, 128), f32),
        ],
        compiler_params=pltpu.CompilerParams(vmem_limit_bytes=WIDE),
        cost_estimate=pl.CostEstimate(
            flops=n * rows * rows * HD * 8, bytes_accessed=n * rows * HD * 10, transcendentals=0
        ),
        name="own",
    )(q, k, v)


def pick(block, lane, h):
    return jnp.max(jnp.where(lane == h, block, NEG), axis=1, keepdims=True)


def anchor_kernel(parts, n_ref, q_ref, *refs):
    k_refs, v_refs = refs[:parts], refs[parts : 2 * parts]
    o_ref, stat_ref, _, out_ref = refs[2 * parts :]
    rows = q_ref.shape[0]
    h = pl.program_id(0)
    lane = lax.broadcasted_iota(jnp.int32, (TM, 128), 1)
    bias = [
        jnp.where(
            lax.broadcasted_iota(jnp.int32, (1, k.shape[0]), 1) + n_ref[2 + p] < n_ref[0], 0.0, NEG
        )
        for p, k in enumerate(k_refs)
    ]
    for i in range(rows // TM):
        at = pl.ds(i * TM, TM)
        q = q_ref[at, :]
        s_parts = [scores(q, k[...]) + b for k, b in zip(k_refs, bias)]
        m, total, o = attend(s_parts, [v[...] for v in v_refs])
        stat = stat_ref[at, :]
        m_own, l_own = pick(stat, lane, h), pick(stat, lane, h + 64)
        top = jnp.maximum(m, m_own)
        wa, wb = jnp.exp2((m - top) * C), jnp.exp2((m_own - top) * C)
        normed = (o * wa + o_ref[at, :] * wb) / (total * wa + l_own * wb)
        row = lax.broadcasted_iota(jnp.int32, (TM, 128), 0) + i * TM
        out_ref[at, :] = jnp.where(row < n_ref[1], normed, 0.0).astype(out_ref.dtype)


def anchor_call(limits, q, halves, own, out, lo, hi):
    rows = q.shape[0]
    n = hi - lo
    kv = halves[0].shape[1] // (2 * HD)
    part = halves[0].shape[0] // 2
    arrays = [halves[0], halves[0], halves[1], halves[1]]
    k_specs = [pl.BlockSpec((part, HD), lambda h, _, p=p: (p % 2, (lo + h) // GROUP)) for p in range(4)]
    v_specs = [
        pl.BlockSpec((part, HD), lambda h, _, p=p: (p % 2, kv + (lo + h) // GROUP)) for p in range(4)
    ]
    in_specs = [
        pl.BlockSpec((rows, HD), lambda h, _: (0, lo + h)),
        *k_specs,
        *v_specs,
        pl.BlockSpec((rows, HD), lambda h, _: (0, h)),
        pl.BlockSpec((rows, 128), lambda h, _: (0, 0)),
        pl.BlockSpec(memory_space=pl.ANY),
    ]
    operands = [limits, q, *arrays, *arrays, *own, q if out is None else out]
    return pl.pallas_call(
        functools.partial(anchor_kernel, 4),
        grid_spec=pltpu.PrefetchScalarGridSpec(
            num_scalar_prefetch=1,
            grid=(n,),
            in_specs=in_specs,
            out_specs=pl.BlockSpec((rows, HD), lambda h, _: (0, lo + h)),
        ),
        out_shape=jax.ShapeDtypeStruct(q.shape, q.dtype),
        input_output_aliases={} if out is None else {len(operands) - 1: 0},
        compiler_params=pltpu.CompilerParams(vmem_limit_bytes=WIDE),
        cost_estimate=pl.CostEstimate(
            flops=n * rows * rows * HD * 12, bytes_accessed=n * rows * HD * 10, transcendentals=0
        ),
        name="anchor",
    )(*operands)


def lanes(rows):
    return lax.broadcasted_iota(jnp.int32, (rows, 128), 1)


def pack_stat(x, heads):
    lane = lanes(x.shape[0])
    hi = x.astype(jnp.bfloat16).astype(jnp.float32)
    mid = (x - hi).astype(jnp.bfloat16).astype(jnp.float32)
    low = x - hi - mid
    out = jnp.where(lane < 2 * heads, pltpu.roll(mid, heads, 1), pltpu.roll(low, 2 * heads, 1))
    return jnp.where(lane < heads, hi, out).astype(jnp.bfloat16)


def unpack_stat(block, heads):
    x = block.astype(jnp.float32)
    return x + pltpu.roll(x, 128 - heads, 1) + pltpu.roll(x, 128 - 2 * heads, 1)


def query_kernel(heads, n_ref, qa_ref, qb_ref, k_ref, v_ref, k2_ref, v2_ref, *outs):
    rows, keys, extra = qa_ref.shape[0], k_ref.shape[0], k2_ref.shape[1]
    bias = jnp.where(lax.broadcasted_iota(jnp.int32, (1, keys), 1) < n_ref[0], 0.0, NEG)
    lane = lanes(rows)
    row = lax.broadcasted_iota(jnp.int32, (rows, extra), 0)
    col = lax.broadcasted_iota(jnp.int32, (rows, extra), 1)
    for i, q_ref in enumerate((qa_ref, qb_ref)):
        seen = (col <= row + n_ref[2 + i]) & (n_ref[1] > 0)
        tops = jnp.zeros((rows, 128), jnp.float32)
        totals = jnp.ones((rows, 128), jnp.float32)
        sent_ref = outs[2] if i == 0 else outs[3]
        for h in range(heads):
            cols = slice(h * HD, (h + 1) * HD)
            at = slice(h // GROUP * HD, (h // GROUP + 1) * HD)
            q = q_ref[:, cols]
            s_parts = [
                scores(q, k_ref[:, at]) + bias,
                jnp.where(seen, scores(q, k2_ref[0, :, at]), NEG),
            ]
            m, total, o = attend(s_parts, [v_ref[:, at], v2_ref[0, :, at]])
            o = o / total
            if i == 0:
                outs[0][:, cols] = o
            else:
                sent_ref[:, cols] = o.astype(sent_ref.dtype)
            tops = jnp.where(lane == h, m, tops)
            totals = jnp.where(lane == h, total, totals)
        lse = tops * C + jnp.log2(totals)
        if i == 0:
            outs[1][...] = lse
        else:
            sent_ref[:, heads * HD :] = pack_stat(lse, heads)


def part_shapes(rows, heads):
    return [
        jax.ShapeDtypeStruct((rows, heads * HD), jnp.float32),
        jax.ShapeDtypeStruct((rows, 128), jnp.float32),
        jax.ShapeDtypeStruct((rows, heads * HD + 128), jnp.bfloat16),
    ]


def query_call(limits, qa, qb, k, v, k2, v2):
    rows, heads = qa.shape[0], qa.shape[1] // HD
    vmem = pl.BlockSpec(memory_space=pltpu.VMEM)

    def kernel(*refs):
        query_kernel(heads, *refs[:7], refs[7], refs[8], None, refs[9])

    return pl.pallas_call(
        kernel,
        in_specs=[pl.BlockSpec(memory_space=pltpu.SMEM)] + [vmem] * 6,
        out_specs=[vmem] * 3,
        out_shape=part_shapes(rows, heads),
        compiler_params=pltpu.CompilerParams(vmem_limit_bytes=VMEM),
        cost_estimate=pl.CostEstimate(
            flops=2 * heads * rows * (k.shape[0] + rows) * HD * 8,
            bytes_accessed=2 * rows * heads * HD * 4,
            transcendentals=0,
        ),
        name="query",
    )(limits, qa, qb, k, v, k2, v2)


def weights_of(lse, other):
    top = jnp.maximum(lse, other)
    wa, wb = jnp.exp2(lse - top), jnp.exp2(other - top)
    both = wa + wb
    return wa / both, wb / both, top + jnp.log2(both)


def merged(wa, wb, o_ref, got_ref, h):
    cols = slice(h * HD, (h + 1) * HD)
    return o_ref[:, cols] * wa[:, h : h + 1] + got_ref[:, cols].astype(jnp.float32) * wb[:, h : h + 1]


def merge_kernel(heads, o_ref, lse_ref, got_ref, *outs):
    wa, wb, lse = weights_of(lse_ref[...], unpack_stat(got_ref[:, heads * HD :], heads))
    for h in range(heads):
        cols = slice(h * HD, (h + 1) * HD)
        o = merged(wa, wb, o_ref, got_ref, h)
        if len(outs) == 3:
            outs[0][:, cols] = o
        outs[-1][:, cols] = o.astype(outs[-1].dtype)
    if len(outs) == 3:
        outs[1][...] = lse
        outs[2][:, heads * HD :] = pack_stat(lse, heads)


def merge_call(o, lse, got, last):
    rows, heads = o.shape[0], o.shape[1] // HD
    vmem = pl.BlockSpec(memory_space=pltpu.VMEM)
    shapes = part_shapes(rows, heads)
    if last:
        shapes = [jax.ShapeDtypeStruct((rows, heads * HD), jnp.bfloat16)]
    return pl.pallas_call(
        functools.partial(merge_kernel, heads),
        in_specs=[vmem] * 3,
        out_specs=[vmem] * len(shapes),
        out_shape=shapes,
        compiler_params=pltpu.CompilerParams(vmem_limit_bytes=VMEM),
        cost_estimate=pl.CostEstimate(flops=1 << 20, bytes_accessed=2 << 20, transcendentals=0),
        name="merge",
    )(o, lse, got)


def project_kernel(n_ref, w_ref, mine_ref, theirs_ref, out_ref):
    rows = mine_ref.shape[0]
    for i, ref in enumerate((mine_ref, theirs_ref)):
        at = pl.ds(pl.multiple_of(n_ref[2 + i], rows), rows)
        out_ref[at, :] = jnp.dot(ref[...], w_ref[...], preferred_element_type=jnp.float32)


def project_call(limits, mine, theirs, w):
    rows = mine.shape[0]
    vmem = pl.BlockSpec(memory_space=pltpu.VMEM)
    return pl.pallas_call(
        project_kernel,
        in_specs=[pl.BlockSpec(memory_space=pltpu.SMEM)] + [vmem] * 3,
        out_specs=vmem,
        out_shape=jax.ShapeDtypeStruct((2 * rows, w.shape[1]), jnp.float32),
        compiler_params=pltpu.CompilerParams(vmem_limit_bytes=VMEM),
        cost_estimate=pl.CostEstimate(
            flops=4 * rows * w.shape[0] * w.shape[1], bytes_accessed=3 << 20, transcendentals=0
        ),
        name="project",
    )(limits, w, mine, theirs)


def per_device(
    grid,
    ctx_q,
    ctx_k,
    ctx_v,
    query_q,
    query_k,
    query_v,
    out_weight,
    anchor_index,
    owner_index,
    counts,
):
    rows = ctx_q.shape[0]
    heads = ctx_q.shape[1] // HD
    me, hid = lax.axis_index("blk"), lax.axis_index("head")
    anchor, owner = anchor_index[0], owner_index[0]
    my_code = code_of(me)
    f32 = jnp.float32

    odd = (hid & 1) == 1

    def side_of(step):
        return (my_code >> grid.bit(step, odd)) & 1

    def far(root, step):
        return ((code_of(root) ^ my_code) >> grid.bit(step, odd)) & 1 == 1

    def hop(x, step):
        return grid.hop(x, step)

    def cut(x, side):
        half = x.shape[0] // 2
        return lax.dynamic_slice_in_dim(x, side * half, half, 0)

    last = grid.dims - 1
    side = side_of(0)
    query = query_q[0]
    q_rows = query.shape[0] // 2
    qa = jnp.where(far(owner, 0), hop(cut(query, 1 - side), 0), cut(query, side))
    for step in range(1, grid.dims):
        qa = jnp.where(far(owner, step), hop(qa, step), qa)
    qb = hop(qa, 0)

    side1 = side_of(1)

    def both(cutter):
        return jnp.concatenate([cutter(ctx_k), cutter(ctx_v)], axis=1)

    mine = jnp.where(
        far(anchor, 0),
        hop(both(lambda x: cut(x, 1 - side)), 0),
        both(lambda x: cut(x, side)),
    )
    mine = jnp.where(far(anchor, 1), hop(cut(mine, 1 - side1), 1), cut(mine, side1))
    for step in range(2, grid.dims):
        mine = jnp.where(far(anchor, step), hop(mine, step), mine)
    mine = jnp.concatenate([mine, hop(mine, 1)], axis=0)
    halves = [mine, hop(mine, 0)]
    part = rows // 4
    starts = [
        2 * part * s0 + part * s1 for s0 in (side, 1 - side) for s1 in (side1, 1 - side1)
    ]

    pieces = 4
    width = heads // pieces
    cuts = [(i * width, (i + 1) * width) for i in range(pieces)]
    own = []
    for a, b in cuts:
        own.append(own_call(ctx_q, ctx_k, ctx_v, a, b))

    q_limits = jnp.stack(
        [counts[me], (me == owner).astype(jnp.int32), side * q_rows, (1 - side) * q_rows]
    )
    o, lse, sent = query_call(q_limits, qa, qb, ctx_k, ctx_v, query_k, query_v)
    for step in range(grid.dims):
        got = hop(sent, step)
        done = merge_call(o, lse, got, step == last)
        if step < last:
            o, lse, sent = done
    theirs = hop(done[0], 0)
    partial = project_call(q_limits, done[0], theirs, out_weight)

    top = partial.shape[0] // 2
    low, high = partial[:top], partial[top:]
    keep, give = jnp.where(odd, high, low), jnp.where(odd, low, high)
    got = grid.head_hop(give, 0)
    total = keep + got
    for bit in range(1, log2_of(grid.n_head)):
        sent = total.astype(jnp.bfloat16)
        got = grid.head_hop(sent, bit)
        total = sent.astype(f32) + got.astype(f32)
    ours = total.astype(jnp.bfloat16)
    rest = grid.head_hop(ours, 0)
    answer = jnp.where(
        odd, jnp.concatenate([rest, ours], axis=0), jnp.concatenate([ours, rest], axis=0)
    )

    limits = jnp.stack([jnp.where(me == anchor, 0, counts[anchor]), counts[me], *starts])
    out = None
    for i, (a, b) in enumerate(cuts):
        out = anchor_call(limits, ctx_q, halves, own[i], out, a, b)
    return out, answer


def solution(mesh):
    placed = (
        P("blk", "head"),
        P("blk", "head"),
        P("blk", "head"),
        P("blk", None, "head"),
        P("blk", None, "head"),
        P("blk", None, "head"),
        P("head", "blk"),
        P(),
        P(),
        P(),
    )
    grid = Grid(mesh.shape["blk"], mesh.shape["head"])

    def whole(*args):
        return per_device(grid, *args)

    return jax.shard_map(
        whole,
        mesh=mesh,
        in_specs=placed,
        out_specs=(P("blk", "head"), P(None, "blk")),
        check_vma=False,
    )
```

profile of v0, /device:TPU:0, one launch (start us, length us, event | category | flops | bytes accessed | tf_op | source)
XLA Modules:
  0.0 113.2 jit_solution(6405936218883872575)
XLA Ops:
  1.7 3.0 %collective-permute-start.5 = (bf16[128,1024]{1,0:T(8,128)(2,1)S(1)}, bf16[128,1024]{1,0:T(8,128)(2,1)S(1)}, u32[]{:S(2)}, u32[]{:S(2)}) collective-permute-start(bf16[128,1024]{1,0:T(8,128)(2,1)S(1)} %dynamic-slice_bitcast_fusion), channel_id=1, source_target_pairs={{0,4},{1,9},{2,6},{3,11},{4,0},{5,13},{6,2},{7,15},{8,12},{9,1},{1... | collective-permute-start | bytes 786440 | tf_op jit(solution)/shard_map/ppermute | solution.py:58
  4.7 1.3 %constant_dynamic-slice_fusion.1 = (bf16[512,256]{1,0:T(8,128)(2,1)S(1)}, bf16[512,256]{1,0:T(8,128)(2,1)S(1)}, bf16[512,256]{1,0:T(8,128)(2,1)S(1)}, bf16[512,256]{1,0:T(8,128)(2,1)S(1)}) fusion(bf16[1024,256]{1,0:T(8,128)(2,1)} %refs_4_.1, s32[]{:T(128)S(6)} %select_n.116, s32[]{:T(128)S(6)} %select_n.115, bf16[1024,256]{1,0:T(8,128)(2,1)} %refs_3_.1), kind=kLoop, calls=%fused_computation.14 | loop fusion | bytes 2097160 | tf_op jit(solution)/shard_map/dynamic_slice | solution.py:391
  7.5 1.6 %collective-permute-done.5 = bf16[128,1024]{1,0:T(8,128)(2,1)S(1)} collective-permute-done((bf16[128,1024]{1,0:T(8,128)(2,1)S(1)}, bf16[128,1024]{1,0:T(8,128)(2,1)S(1)}, u32[]{:S(2)}, u32[]{:S(2)}) %collective-permute-start.5) | collective-permute-done | bytes 262176 | tf_op jit(solution)/shard_map/ppermute | solution.py:58
  9.1 2.2 %collective-permute-start.6 = (bf16[128,1024]{1,0:T(8,128)(2,1)S(1)}, bf16[128,1024]{1,0:T(8,128)(2,1)S(1)}, u32[]{:S(2)}, u32[]{:S(2)}) collective-permute-start(bf16[128,1024]{1,0:T(8,128)(2,1)S(1)} %bitcast_select_fusion), channel_id=1, source_target_pairs={{0,8},{1,25},{2,10},{3,27},{4,12},{5,29},{6,14},{7,31},{8,0},{9,17... | collective-permute-start | bytes 786440 | tf_op jit(solution)/shard_map/ppermute | solution.py:58
  12.0 6.0 %collective-permute-done.6 = bf16[128,1024]{1,0:T(8,128)(2,1)S(1)} collective-permute-done((bf16[128,1024]{1,0:T(8,128)(2,1)S(1)}, bf16[128,1024]{1,0:T(8,128)(2,1)S(1)}, u32[]{:S(2)}, u32[]{:S(2)}) %collective-permute-start.6) | collective-permute-done | bytes 262176 | tf_op jit(solution)/shard_map/ppermute | solution.py:58
  18.0 5.4 %collective-permute-start.7 = (bf16[128,1024]{1,0:T(8,128)(2,1)S(1)}, bf16[128,1024]{1,0:T(8,128)(2,1)}, u32[]{:S(2)}, u32[]{:S(2)}) collective-permute-start(bf16[128,1024]{1,0:T(8,128)(2,1)S(1)} %broadcast_select_fusion), channel_id=1, source_target_pairs={{0,24},{1,5},{2,26},{3,7},{4,28},{5,1},{6,30},{7,3},{8,16},{9,13},... | collective-permute-start | bytes 786440 | tf_op jit(solution)/shard_map/ppermute | solution.py:58
  23.4 1.2 %maximum_select_fusion = bf16[512,512]{1,0:T(8,128)(2,1)S(1)} fusion(bf16[512,512]{1,0:T(8,128)(2,1)} %collective-permute-done, bf16[512,256]{1,0:T(8,128)(2,1)S(1)} %get-tuple-element.38, bf16[512,256]{1,0:T(8,128)(2,1)S(1)} %get-tuple-element.43, pred[]{:T(512)S(6)} %eq.31), kind=kLoop, calls=%fused_computation.1 | loop fusion | flops 1310720 | bytes 1572865 | tf_op jit(solution)/shard_map/jit(_where)/select_n | solution.py:407
  25.4 4.6 %collective-permute-done.7 = bf16[128,1024]{1,0:T(8,128)(2,1)} collective-permute-done((bf16[128,1024]{1,0:T(8,128)(2,1)S(1)}, bf16[128,1024]{1,0:T(8,128)(2,1)}, u32[]{:S(2)}, u32[]{:S(2)}) %collective-permute-start.7) | collective-permute-done | bytes 262176 | tf_op jit(solution)/shard_map/ppermute | solution.py:58
  31.0 4.6 %collective-permute-done.1 = bf16[256,512]{1,0:T(8,128)(2,1)S(1)} collective-permute-done((bf16[256,512]{1,0:T(8,128)(2,1)S(1)}, bf16[256,512]{1,0:T(8,128)(2,1)S(1)}, u32[]{:S(2)}, u32[]{:S(2)}) %collective-permute-start.1) | collective-permute-done | bytes 262176 | tf_op jit(solution)/shard_map/ppermute | solution.py:58
  35.7 3.4 %collective-permute-start.2 = (bf16[256,512]{1,0:T(8,128)(2,1)S(1)}, bf16[256,512]{1,0:T(8,128)(2,1)S(1)}, u32[]{:S(2)}, u32[]{:S(2)}) collective-permute-start(bf16[256,512]{1,0:T(8,128)(2,1)S(1)} %dynamic-slice_select_fusion), channel_id=1, source_target_pairs={{0,24},{1,5},{2,26},{3,7},{4,28},{5,1},{6,30},{7,3},{8,16},{9,13},... | collective-permute-start | bytes 786440 | tf_op jit(solution)/shard_map/ppermute | solution.py:58
  39.8 4.6 %query.1 = (f32[128,1024]{1,0:T(8,128)S(1)}, f32[128,128]{1,0:T(8,128)S(1)}, bf16[128,1152]{1,0:T(8,128)(2,1)S(1)}) custom-call(s32[4]{0:T(128)S(1)} %pad_add_fusion.refs_0_.n_ref, bf16[128,1024]{1,0:T(8,128)(2,1)S(1)} %broadcast_select_fusion.1.refs_1_, bf16[128,1024]{1,0:T(8,128)(2,1)S(1)} %collective-permute-done.8.refs_2_, ...), custom_call_target="tpu_custom_call" | custom-call | flops 2415919104 | bytes 1048576 | tf_op jit(solution)/shard_map/query/pallas_call | solution.py:278
  44.7 3.9 %collective-permute-start.3 = (bf16[256,512]{1,0:T(8,128)(2,1)S(1)}, bf16[256,512]{1,0:T(8,128)(2,1)S(1)}, u32[]{:S(2)}, u32[]{:S(2)}) collective-permute-start(bf16[256,512]{1,0:T(8,128)(2,1)S(1)} %broadcast_select_fusion.2), channel_id=1, source_target_pairs={{0,8},{1,25},{2,10},{3,27},{4,12},{5,29},{6,14},{7,31},{8,0},{9,17... | collective-permute-start | bytes 786440 | tf_op jit(solution)/shard_map/ppermute | solution.py:58
  48.6 5.7 %own.7 = (f32[1024,256]{1,0:T(8,128)}, f32[1024,128]{1,0:T(8,128)}) custom-call(bf16[1024,1024]{1,0:T(8,128)(2,1)} %q_ref.15, bf16[1024,256]{1,0:T(8,128)(2,1)} %refs_3_.1, bf16[1024,256]{1,0:T(8,128)(2,1)} %refs_4_.1), custom_call_target="tpu_custom_call" | custom-call | flops 2147483648 | bytes 2621440 | tf_op jit(solution)/shard_map/own/pallas_call | solution.py:120
  55.7 5.7 %own.6 = (f32[1024,256]{1,0:T(8,128)}, f32[1024,128]{1,0:T(8,128)}) custom-call(bf16[1024,1024]{1,0:T(8,128)(2,1)} %q_ref.15, bf16[1024,256]{1,0:T(8,128)(2,1)} %refs_3_.1, bf16[1024,256]{1,0:T(8,128)(2,1)} %refs_4_.1), custom_call_target="tpu_custom_call" | custom-call | flops 2147483648 | bytes 2621440 | tf_op jit(solution)/shard_map/own/pallas_call | solution.py:120
  61.4 3.3 %collective-permute-done.10.got_ref = bf16[128,1152]{1,0:T(8,128)(2,1)S(1)} collective-permute-done((bf16[128,1152]{1,0:T(8,128)(2,1)S(1)}, bf16[128,1152]{1,0:T(8,128)(2,1)S(1)}, u32[]{:S(2)}, u32[]{:S(2)}) %collective-permute-start.10) | collective-permute-done | bytes 294944 | tf_op jit(solution)/shard_map/ppermute | solution.py:58
  65.2 1.9 %collective-permute-start.11 = (bf16[128,1152]{1,0:T(8,128)(2,1)S(1)}, bf16[128,1152]{1,0:T(8,128)(2,1)S(1)}, u32[]{:S(2)}, u32[]{:S(2)}) collective-permute-start(bf16[128,1152]{1,0:T(8,128)(2,1)S(1)} %get-tuple-element.35), channel_id=1, source_target_pairs={{0,24},{1,5},{2,26},{3,7},{4,28},{5,1},{6,30},{7,3},{8,16},{9,13},... | collective-permute-start | bytes 884744 | tf_op jit(solution)/shard_map/ppermute | solution.py:58
  67.1 5.7 %own.5 = (f32[1024,256]{1,0:T(8,128)}, f32[1024,128]{1,0:T(8,128)}) custom-call(bf16[1024,1024]{1,0:T(8,128)(2,1)} %q_ref.15, bf16[1024,256]{1,0:T(8,128)(2,1)} %refs_3_.1, bf16[1024,256]{1,0:T(8,128)(2,1)} %refs_4_.1), custom_call_target="tpu_custom_call" | custom-call | flops 2147483648 | bytes 2621440 | tf_op jit(solution)/shard_map/own/pallas_call | solution.py:120
  73.5 1.3 %stack.38.n_ref = s32[6]{0:T(128)} concatenate(s32[1]{0:T(128)} %bitcast.2, s32[1]{0:T(128)} %get-tuple-element.40, s32[1]{0:T(128)} %bitcast.3, s32[1]{0:T(128)} %bitcast.4, s32[1]{0:T(128)} %bitcast.5, s32[1]{0:T(128)} %bitcast.6), dimensions={0} | concatenate | bytes 48 | tf_op jit(solution)/shard_map/stack | solution.py:456
  74.8 5.7 %own.4 = (f32[1024,256]{1,0:T(8,128)}, f32[1024,128]{1,0:T(8,128)}) custom-call(bf16[1024,1024]{1,0:T(8,128)(2,1)} %q_ref.15, bf16[1024,256]{1,0:T(8,128)(2,1)} %refs_3_.1, bf16[1024,256]{1,0:T(8,128)(2,1)} %refs_4_.1), custom_call_target="tpu_custom_call" | custom-call | flops 2147483648 | bytes 2621440 | tf_op jit(solution)/shard_map/own/pallas_call | solution.py:120
  81.5 7.0 %anchor.4.refs_10_ = bf16[1024,1024]{1,0:T(8,128)(2,1)} custom-call(s32[6]{0:T(128)} %stack.38.n_ref, bf16[1024,1024]{1,0:T(8,128)(2,1)} %q_ref.15, bf16[512,512]{1,0:T(8,128)(2,1)} %copy-done.5, bf16[512,512]{1,0:T(8,128)(2,1)} %copy-done.5, bf16[512,512]{1,0:T(8,128)(2,1)} %collective-permute-done.4.refs_2_.refs_3_.refs_6_.refs_7_, ...), custom_call_target="tpu_custom_call" | custom-call | flops 3221225472 | bytes 2621440 | tf_op jit(solution)/shard_map/anchor/pallas_call | solution.py:193
  89.7 6.9 %anchor.5.refs_10_ = bf16[1024,1024]{1,0:T(8,128)(2,1)} custom-call(s32[6]{0:T(128)} %stack.38.n_ref, bf16[1024,1024]{1,0:T(8,128)(2,1)} %q_ref.15, bf16[512,512]{1,0:T(8,128)(2,1)} %copy-done.5, bf16[512,512]{1,0:T(8,128)(2,1)} %copy-done.5, ...), custom_call_target="tpu_custom_call", output_to_operand_aliasing={{}: (12, {})} | custom-call | flops 3221225472 | bytes 2621440 | tf_op jit(solution)/shard_map/anchor/pallas_call | solution.py:193
  96.7 1.6 %collective-permute-start.14 = (bf16[128,512]{1,0:T(8,128)(2,1)S(1)}, bf16[128,512]{1,0:T(8,128)(2,1)S(1)}, u32[]{:S(2)}, u32[]{:S(2)}) collective-permute-start(bf16[128,512]{1,0:T(8,128)(2,1)S(1)} %add_convert_fusion.1), channel_id=1, source_target_pairs={{0,2},{1,3},{2,0},{3,1},{4,6},{5,7},{6,4},{7,5},{8,10},{9,11},{10,... | collective-permute-start | bytes 393224 | tf_op jit(solution)/shard_map/ppermute | solution.py:61
  98.3 6.9 %anchor.6.refs_10_ = bf16[1024,1024]{1,0:T(8,128)(2,1)} custom-call(s32[6]{0:T(128)} %stack.38.n_ref, bf16[1024,1024]{1,0:T(8,128)(2,1)} %q_ref.15, bf16[512,512]{1,0:T(8,128)(2,1)} %copy-done.5, bf16[512,512]{1,0:T(8,128)(2,1)} %copy-done.5, ...), custom_call_target="tpu_custom_call", output_to_operand_aliasing={{}: (12, {})} | custom-call | flops 3221225472 | bytes 2621440 | tf_op jit(solution)/shard_map/anchor/pallas_call | solution.py:193
  105.5 6.9 %anchor.7 = bf16[1024,1024]{1,0:T(8,128)(2,1)} custom-call(s32[6]{0:T(128)} %stack.38.n_ref, bf16[1024,1024]{1,0:T(8,128)(2,1)} %q_ref.15, bf16[512,512]{1,0:T(8,128)(2,1)} %copy-done.5, bf16[512,512]{1,0:T(8,128)(2,1)} %copy-done.5, bf16[512,512]{1,0:T(8,128)(2,1)} %collective-permute-done.4.refs_2_.refs_3_.refs_6_.refs_7_, ...), custom_call_target="tpu_custom_call", output_to_operand_aliasing={{}: (12, {})} | custom-call | flops 3221225472 | bytes 2621440 | tf_op jit(solution)/shard_map/anchor/pallas_call | solution.py:193
  (55 shorter events, 10.0 us)
Async XLA Ops:
  0.6 8.4 %copy-start.6 = (bf16[1,256,1024]{2,1,0:T(8,128)(2,1)S(1)}, bf16[1,256,1024]{2,1,0:T(8,128)(2,1)}, u32[]{:S(2)}) copy-start(bf16[1,256,1024]{2,1,0:T(8,128)(2,1)} %param.13) | copy-start | bytes 1572868
  1.7 7.4 %collective-permute-start.5 = (bf16[128,1024]{1,0:T(8,128)(2,1)S(1)}, bf16[128,1024]{1,0:T(8,128)(2,1)S(1)}, u32[]{:S(2)}, u32[]{:S(2)}) collective-permute-start(bf16[128,1024]{1,0:T(8,128)(2,1)S(1)} %dynamic-slice_bitcast_fusion), channel_id=1, source_target_pairs={{0,4},{1,9},{2,6},{3,11},{4,0},{5,13},{6,2},{7,15},{8,12},{9,1},{1... | collective-permute-start | bytes 786440 | tf_op jit(solution)/shard_map/ppermute | solution.py:58
  6.8 17.9 %copy-start.7 = (s32[8]{0:T(128)S(1)}, s32[8]{0:T(128)}, u32[]{:S(2)}) copy-start(s32[8]{0:T(128)} %param.19) | copy-start | bytes 100
  6.8 16.6 %collective-permute-start = (bf16[512,512]{1,0:T(8,128)(2,1)}, bf16[512,512]{1,0:T(8,128)(2,1)}, u32[]{:S(2)}, u32[]{:S(2)}) collective-permute-start(bf16[512,512]{1,0:T(8,128)(2,1)} %pad_maximum_fusion), channel_id=1, source_target_pairs={{0,4},{1,9},{2,6},{3,11},{4,0},{5,13},{6,2},{7,15},{8,12},{9,1},{1... | collective-permute-start | bytes 1572872 | tf_op jit(solution)/shard_map/ppermute | solution.py:58
  9.1 8.9 %collective-permute-start.6 = (bf16[128,1024]{1,0:T(8,128)(2,1)S(1)}, bf16[128,1024]{1,0:T(8,128)(2,1)S(1)}, u32[]{:S(2)}, u32[]{:S(2)}) collective-permute-start(bf16[128,1024]{1,0:T(8,128)(2,1)S(1)} %bitcast_select_fusion), channel_id=1, source_target_pairs={{0,8},{1,25},{2,10},{3,27},{4,12},{5,29},{6,14},{7,31},{8,0},{9,17... | collective-permute-start | bytes 786440 | tf_op jit(solution)/shard_map/ppermute | solution.py:58
  12.0 27.8 %copy-start.1 = (bf16[1024,256]{1,0:T(8,128)(2,1)S(1)}, bf16[1024,256]{1,0:T(8,128)(2,1)}, u32[]{:S(2)}) copy-start(bf16[1024,256]{1,0:T(8,128)(2,1)} %refs_4_.1) | copy-start | bytes 1572868
  12.0 27.8 %copy-start.2 = (bf16[1024,256]{1,0:T(8,128)(2,1)S(1)}, bf16[1024,256]{1,0:T(8,128)(2,1)}, u32[]{:S(2)}) copy-start(bf16[1024,256]{1,0:T(8,128)(2,1)} %refs_3_.1) | copy-start | bytes 1572868
  12.0 27.8 %copy-start.3 = (bf16[1,256,256]{2,1,0:T(8,128)(2,1)S(1)}, bf16[1,256,256]{2,1,0:T(8,128)(2,1)}, u32[]{:S(2)}) copy-start(bf16[1,256,256]{2,1,0:T(8,128)(2,1)} %refs_5_.1) | copy-start | bytes 393220
  12.0 27.8 %copy-start.4 = (bf16[1,256,256]{2,1,0:T(8,128)(2,1)S(1)}, bf16[1,256,256]{2,1,0:T(8,128)(2,1)}, u32[]{:S(2)}) copy-start(bf16[1,256,256]{2,1,0:T(8,128)(2,1)} %refs_6_.1) | copy-start | bytes 393220
  18.0 11.9 %collective-permute-start.7 = (bf16[128,1024]{1,0:T(8,128)(2,1)S(1)}, bf16[128,1024]{1,0:T(8,128)(2,1)}, u32[]{:S(2)}, u32[]{:S(2)}) collective-permute-start(bf16[128,1024]{1,0:T(8,128)(2,1)S(1)} %broadcast_select_fusion), channel_id=1, source_target_pairs={{0,24},{1,5},{2,26},{3,7},{4,28},{5,1},{6,30},{7,3},{8,16},{9,13},... | collective-permute-start | bytes 786440 | tf_op jit(solution)/shard_map/ppermute | solution.py:58
  24.6 11.0 %collective-permute-start.1 = (bf16[256,512]{1,0:T(8,128)(2,1)S(1)}, bf16[256,512]{1,0:T(8,128)(2,1)S(1)}, u32[]{:S(2)}, u32[]{:S(2)}) collective-permute-start(bf16[256,512]{1,0:T(8,128)(2,1)S(1)} %constant_dynamic-slice_fusion), channel_id=1, source_target_pairs={{0,8},{1,25},{2,10},{3,27},{4,12},{5,29},{6,14},{7,31},{8,0},{9,17... | collective-permute-start | bytes 786440 | tf_op jit(solution)/shard_map/ppermute | solution.py:58
  30.0 9.8 %collective-permute-start.8 = (bf16[128,1024]{1,0:T(8,128)(2,1)S(1)}, bf16[128,1024]{1,0:T(8,128)(2,1)S(1)}, u32[]{:S(2)}, u32[]{:S(2)}) collective-permute-start(bf16[128,1024]{1,0:T(8,128)(2,1)S(1)} %broadcast_select_fusion.1.refs_1_), channel_id=1, source_target_pairs={{0,4},{1,9},{2,6},{3,11},{4,0},{5,13},{6,2},{7,15},{8,12},{9,1},{1... | collective-permute-start | bytes 786440 | tf_op jit(solution)/shard_map/ppermute | solution.py:58
  35.7 9.0 %collective-permute-start.2 = (bf16[256,512]{1,0:T(8,128)(2,1)S(1)}, bf16[256,512]{1,0:T(8,128)(2,1)S(1)}, u32[]{:S(2)}, u32[]{:S(2)}) collective-permute-start(bf16[256,512]{1,0:T(8,128)(2,1)S(1)} %dynamic-slice_select_fusion), channel_id=1, source_target_pairs={{0,24},{1,5},{2,26},{3,7},{4,28},{5,1},{6,30},{7,3},{8,16},{9,13},... | collective-permute-start | bytes 786440 | tf_op jit(solution)/shard_map/ppermute | solution.py:58
  44.4 9.9 %collective-permute-start.9 = (bf16[128,1152]{1,0:T(8,128)(2,1)S(1)}, bf16[128,1152]{1,0:T(8,128)(2,1)S(1)}, u32[]{:S(2)}, u32[]{:S(2)}) collective-permute-start(bf16[128,1152]{1,0:T(8,128)(2,1)S(1)} %get-tuple-element.29), channel_id=1, source_target_pairs={{0,4},{1,9},{2,6},{3,11},{4,0},{5,13},{6,2},{7,15},{8,12},{9,1},{1... | collective-permute-start | bytes 884744 | tf_op jit(solution)/shard_map/ppermute | solution.py:58
  44.7 10.4 %collective-permute-start.3 = (bf16[256,512]{1,0:T(8,128)(2,1)S(1)}, bf16[256,512]{1,0:T(8,128)(2,1)S(1)}, u32[]{:S(2)}, u32[]{:S(2)}) collective-permute-start(bf16[256,512]{1,0:T(8,128)(2,1)S(1)} %broadcast_select_fusion.2), channel_id=1, source_target_pairs={{0,8},{1,25},{2,10},{3,27},{4,12},{5,29},{6,14},{7,31},{8,0},{9,17... | collective-permute-start | bytes 786440 | tf_op jit(solution)/shard_map/ppermute | solution.py:58
  54.8 9.9 %collective-permute-start.10 = (bf16[128,1152]{1,0:T(8,128)(2,1)S(1)}, bf16[128,1152]{1,0:T(8,128)(2,1)S(1)}, u32[]{:S(2)}, u32[]{:S(2)}) collective-permute-start(bf16[128,1152]{1,0:T(8,128)(2,1)S(1)} %get-tuple-element.32), channel_id=1, source_target_pairs={{0,8},{1,25},{2,10},{3,27},{4,12},{5,29},{6,14},{7,31},{8,0},{9,17... | collective-permute-start | bytes 884744 | tf_op jit(solution)/shard_map/ppermute | solution.py:58
  55.1 6.3 %copy-start.5 = (bf16[512,512]{1,0:T(8,128)(2,1)}, bf16[512,512]{1,0:T(8,128)(2,1)S(1)}, u32[]{:S(2)}) copy-start(bf16[512,512]{1,0:T(8,128)(2,1)S(1)} %pad_maximum_fusion.1.refs_0_.refs_1_.refs_4_.refs_5_) | copy-start | bytes 1572868
  55.1 26.4 %collective-permute-start.4 = (bf16[512,512]{1,0:T(8,128)(2,1)S(1)}, bf16[512,512]{1,0:T(8,128)(2,1)}, u32[]{:S(2)}, u32[]{:S(2)}) collective-permute-start(bf16[512,512]{1,0:T(8,128)(2,1)S(1)} %pad_maximum_fusion.1.refs_0_.refs_1_.refs_4_.refs_5_), channel_id=1, source_target_pairs={{0,4},{1,9},{2,6},{3,11},{4,0},{5,13},{6,2},{7,15},{8,12},{9,1},{1... | collective-permute-start | bytes 1572872 | tf_op jit(solution)/shard_map/ppermute | solution.py:58
  65.2 15.3 %collective-permute-start.11 = (bf16[128,1152]{1,0:T(8,128)(2,1)S(1)}, bf16[128,1152]{1,0:T(8,128)(2,1)S(1)}, u32[]{:S(2)}, u32[]{:S(2)}) collective-permute-start(bf16[128,1152]{1,0:T(8,128)(2,1)S(1)} %get-tuple-element.35), channel_id=1, source_target_pairs={{0,24},{1,5},{2,26},{3,7},{4,28},{5,1},{6,30},{7,3},{8,16},{9,13},... | collective-permute-start | bytes 884744 | tf_op jit(solution)/shard_map/ppermute | solution.py:58
  81.0 7.6 %collective-permute-start.12 = (bf16[128,1024]{1,0:T(8,128)(2,1)S(1)}, bf16[128,1024]{1,0:T(8,128)(2,1)S(1)}, u32[]{:S(2)}, u32[]{:S(2)}) collective-permute-start(bf16[128,1024]{1,0:T(8,128)(2,1)S(1)} %merge.5.mine_ref), channel_id=1, source_target_pairs={{0,4},{1,9},{2,6},{3,11},{4,0},{5,13},{6,2},{7,15},{8,12},{9,1},{1... | collective-permute-start | bytes 786440 | tf_op jit(solution)/shard_map/ppermute | solution.py:58
  81.5 7.1 %copy-start = (bf16[1024,512]{1,0:T(8,128)(2,1)S(1)}, bf16[1024,512]{1,0:T(8,128)(2,1)}, u32[]{:S(2)}) copy-start(bf16[1024,512]{1,0:T(8,128)(2,1)} %w_ref.1) | copy-start | bytes 3145732
  89.6 7.0 %collective-permute-start.13 = (f32[128,512]{1,0:T(8,128)S(1)}, f32[128,512]{1,0:T(8,128)S(1)}, u32[]{:S(2)}, u32[]{:S(2)}) collective-permute-start(f32[128,512]{1,0:T(8,128)S(1)} %slice_select_fusion), channel_id=1, source_target_pairs={{0,1},{1,0},{2,3},{3,2},{4,5},{5,4},{6,7},{7,6},{8,9},{9,8},{10,11... | collective-permute-start | bytes 786440 | tf_op jit(solution)/shard_map/ppermute | solution.py:61
  96.7 8.5 %collective-permute-start.14 = (bf16[128,512]{1,0:T(8,128)(2,1)S(1)}, bf16[128,512]{1,0:T(8,128)(2,1)S(1)}, u32[]{:S(2)}, u32[]{:S(2)}) collective-permute-start(bf16[128,512]{1,0:T(8,128)(2,1)S(1)} %add_convert_fusion.1), channel_id=1, source_target_pairs={{0,2},{1,3},{2,0},{3,1},{4,6},{5,7},{6,4},{7,5},{8,10},{9,11},{10,... | collective-permute-start | bytes 393224 | tf_op jit(solution)/shard_map/ppermute | solution.py:61
  105.2 7.2 %collective-permute-start.15 = (bf16[128,512]{1,0:T(8,128)(2,1)S(1)}, bf16[128,512]{1,0:T(8,128)(2,1)S(1)}, u32[]{:S(2)}, u32[]{:S(2)}) collective-permute-start(bf16[128,512]{1,0:T(8,128)(2,1)S(1)} %add_convert_fusion), channel_id=1, source_target_pairs={{0,1},{1,0},{2,3},{3,2},{4,5},{5,4},{6,7},{7,6},{8,9},{9,8},{10,11... | collective-permute-start | bytes 393224 | tf_op jit(solution)/shard_map/ppermute | solution.py:61
where the time goes:
time: 114 us; the launch traced here: 113 us
  Pallas kernels  57.6 us (51%)
  starting transfers between devices  24.5 us (21%)
  waiting for transfers between devices  20.1 us (18%)
  local copies, waits for them, and re-layouts  4.29 us (4%)
  other arithmetic  3.88 us (3%)
  between operations  2.93 us (3%)
    pallas_call x4, Pallas kernels, anchor_call(): pl.pallas_call(functools.partial(anchor_kernel, 4), grid_spec=pltpu.Prefe...  27.8 us
    pallas_call x4, Pallas kernels, own_call(): pl.pallas_call(own_kernel, grid=(n,), in_specs=[pl.BlockSpec((rows, HD),...  22.8 us
    ppermute x13, starting transfers between devices, hop(): return lax.ppermute(value, ('blk', 'head'), pairs)  22.5 us
    ppermute x13, waiting for transfers between devices, hop(): return lax.ppermute(value, ('blk', 'head'), pairs)  20.1 us
    pallas_call x1, Pallas kernels, query_call(): pl.pallas_call(kernel, in_specs=[pl.BlockSpec(memory_space=pltpu.SMEM)] +...  4.55 us
    dynamic_slice x3, local copies, waits for them, and re-layouts, cut(): return lax.dynamic_slice_in_dim(x, side * half, half, 0)  2.31 us
  transfers between devices with their start and end apart: 16, of which 5 were waited for; matrix products, arithmetic and copies ran while one was open for 5% of the time, Pallas kernels for 50%

commit v1 on v0

--- a/solution.py
+++ b/solution.py
@@ -17,8 +17,8 @@
 NEG = -1e30
 NT = (((1,), (1,)), ((), ()))
 TM = 256
-VMEM = 14 << 20
-WIDE = 61 << 20
+VMEM = 8 << 20
+WIDE = 8 << 20
 
 
 def code_of(i):
@@ -62,28 +62,28 @@
 
 
 def scores(q, k):
-    return lax.dot_general(q, k, NT, preferred_element_type=jnp.float32)
-
-
-def lane_max(s):
-    m = s[:, :128]
-    for j in range(1, s.shape[1] // 128):
-        m = jnp.maximum(m, s[:, j * 128 : (j + 1) * 128])
+    return lax.dot_general(q, k, NT, preferred_element_type=jnp.float32) * C
+
+
+def top_of(s_parts):
+    m = None
+    for s in s_parts:
+        for j in range(s.shape[1] // 128):
+            x = s[:, j * 128 : (j + 1) * 128]
+            m = x if m is None else jnp.maximum(m, x)
     return jnp.max(m, axis=1, keepdims=True)
 
 
-def weigh(p, v):
-    wide = jnp.concatenate([v, jnp.ones_like(v)], axis=1)
-    both = jnp.dot(p.astype(jnp.bfloat16), wide, preferred_element_type=jnp.float32)
-    return both
-
-
-def attend(s_parts, v_parts):
-    m = functools.reduce(jnp.maximum, [lane_max(s) for s in s_parts])
-    mc = m * C
+def wide(v):
+    return jnp.concatenate([v, jnp.ones_like(v)], axis=1)
+
+
+def attend(s_parts, wide_parts):
+    m = top_of(s_parts)
     acc = None
-    for s, v in zip(s_parts, v_parts):
-        both = weigh(jnp.exp2(s * C - mc), v)
+    for s, v in zip(s_parts, wide_parts):
+        p = jnp.exp2(s - m).astype(jnp.bfloat16)
+        both = jnp.dot(p, v, preferred_element_type=jnp.float32)
         acc = both if acc is None else acc + both
     return m, acc[:, HD:], acc[:, :HD]
 
@@ -94,115 +94,186 @@
     return c <= r
 
 
-def own_kernel(q_ref, k_ref, v_ref, o_ref, stat_ref):
+def own_kernel(lo, q_ref, k_ref, v_ref, *refs):
+    o_ref, stat_ref = refs[-2:]
     rows = q_ref.shape[0]
     h = pl.program_id(0)
-    lane = lax.broadcasted_iota(jnp.int32, (TM, 128), 1)
+    lane = lanes(TM)
+
+    if len(refs) == 4:
+
+        @pl.when(h == 0)
+        def _():
+            stat_ref[...] = refs[1][...]
+
+    def score(i):
+        q = q_ref[i * TM : (i + 1) * TM, :]
+        parts = [scores(q, k_ref[j * TM : (j + 1) * TM, :]) for j in range(i)]
+        diagonal = scores(q, k_ref[i * TM : (i + 1) * TM, :])
+        return parts + [jnp.where(causal(TM, TM, 0), diagonal, NEG)]
+
+    ready = score(0)
     for i in range(rows // TM):
         at = pl.ds(i * TM, TM)
-        q = q_ref[at, :]
-        n = i * TM
-        s_parts = [jnp.where(causal(TM, TM, 0), scores(q, k_ref[at, :]), NEG)]
-        v_parts = [v_ref[at, :]]
-        if n:
-            s_parts.append(scores(q, k_ref[:n, :]))
-            v_parts.append(v_ref[:n, :])
-        m, total, o = attend(s_parts, v_parts)
+        s_parts = ready
+        if (i + 1) * TM < rows:
+            ready = score(i + 1)
+        m, total, o = attend(s_parts, [wide(v_ref[j * TM : (j + 1) * TM, :]) for j in range(i + 1)])
         o_ref[at, :] = o
-        stat = jnp.where(lane == h, m, stat_ref[at, :])
-        stat_ref[at, :] = jnp.where(lane == h + 64, total, stat)
-
-
-def own_call(q, k, v, lo, hi):
+        put_stat(stat_ref, at, lane, lo + h, m, total)
+
+
+def put_stat(ref, at, lane, h, m, total):
+    stat = jnp.where(lane == h, m, ref[at, :])
+    ref[at, :] = jnp.where(lane == h + 64, total, stat)
+
+
+def state_shapes(q):
+    return [
+        jax.ShapeDtypeStruct(q.shape, jnp.float32),
+        jax.ShapeDtypeStruct((q.shape[0], 128), jnp.float32),
+    ]
+
+
+def own_call(q, k, v, state, lo, hi):
     rows = q.shape[0]
     n = hi - lo
-    f32 = jnp.float32
+    head = pl.BlockSpec((rows, HD), lambda h: (0, lo + h))
+    stat = pl.BlockSpec((rows, 128), lambda h: (0, 0))
+    group = pl.BlockSpec((rows, HD), lambda h: (0, (lo + h) // GROUP))
+    more = [] if state is None else [pl.BlockSpec(memory_space=pl.ANY), stat]
     return pl.pallas_call(
-        own_kernel,
+        functools.partial(own_kernel, lo),
         grid=(n,),
-        in_specs=[
-            pl.BlockSpec((rows, HD), lambda h: (0, lo + h)),
-            pl.BlockSpec((rows, HD), lambda h: (0, (lo + h) // GROUP)),
-            pl.BlockSpec((rows, HD), lambda h: (0, (lo + h) // GROUP)),
-        ],
-        out_specs=[
-            pl.BlockSpec((rows, HD), lambda h: (0, h)),
-            pl.BlockSpec((rows, 128), lambda h: (0, 0)),
-        ],
-        out_shape=[
-            jax.ShapeDtypeStruct((rows, n * HD), f32),
-            jax.ShapeDtypeStruct((rows, 128), f32),
-        ],
+        in_specs=[head, group, group, *more],
+        out_specs=[head, stat],
+        out_shape=state_shapes(q),
+        input_output_aliases={} if state is None else {3: 0, 4: 1},
         compiler_params=pltpu.CompilerParams(vmem_limit_bytes=WIDE),
         cost_estimate=pl.CostEstimate(
             flops=n * rows * rows * HD * 8, bytes_accessed=n * rows * HD * 10, transcendentals=0
         ),
         name="own",
-    )(q, k, v)
+    )(q, k, v, *([] if state is None else state))
 
 
 def pick(block, lane, h):
     return jnp.max(jnp.where(lane == h, block, NEG), axis=1, keepdims=True)
 
 
-def anchor_kernel(parts, n_ref, q_ref, *refs):
+def anchor_kernel(lo, parts, seen_at, final, n_ref, q_ref, *refs):
     k_refs, v_refs = refs[:parts], refs[parts : 2 * parts]
-    o_ref, stat_ref, _, out_ref = refs[2 * parts :]
-    rows = q_ref.shape[0]
+    o_ref, stat_ref = refs[2 * parts : 2 * parts + 2]
+    k_all, v_all = refs[-2:]
+    outs = refs[2 * parts + (3 if final else 2) : -2]
+    rows, part = q_ref.shape[0], k_refs[0].shape[0]
     h = pl.program_id(0)
-    lane = lax.broadcasted_iota(jnp.int32, (TM, 128), 1)
-    bias = [
-        jnp.where(
-            lax.broadcasted_iota(jnp.int32, (1, k.shape[0]), 1) + n_ref[2 + p] < n_ref[0], 0.0, NEG
-        )
-        for p, k in enumerate(k_refs)
-    ]
-    for i in range(rows // TM):
+    lane = lanes(TM)
+    seen = n_ref[seen_at]
+
+    @pl.when((h == 0) | ((lo + h) % GROUP == 0))
+    def _():
+        for p in range(parts):
+            at = pl.ds(pl.multiple_of(n_ref[seen_at + 1 + p], part), part)
+            k_all[at, :] = k_refs[p][...]
+            v_all[at, :] = wide(v_refs[p][...])
+
+    if not final:
+
+        @pl.when(h == 0)
+        def _():
+            outs[1][...] = stat_ref[...]
+
+    def store(i, m, total, o):
         at = pl.ds(i * TM, TM)
-        q = q_ref[at, :]
-        s_parts = [scores(q, k[...]) + b for k, b in zip(k_refs, bias)]
-        m, total, o = attend(s_parts, [v[...] for v in v_refs])
         stat = stat_ref[at, :]
-        m_own, l_own = pick(stat, lane, h), pick(stat, lane, h + 64)
+        m_own, l_own = pick(stat, lane, lo + h), pick(stat, lane, lo + h + 64)
         top = jnp.maximum(m, m_own)
-        wa, wb = jnp.exp2((m - top) * C), jnp.exp2((m_own - top) * C)
-        normed = (o * wa + o_ref[at, :] * wb) / (total * wa + l_own * wb)
+        wa, wb = jnp.exp2(m - top), jnp.exp2(m_own - top)
+        both, l_both = o * wa + o_ref[at, :] * wb, total * wa + l_own * wb
+        if final:
+            finish(i, both, l_both)
+        else:
+            outs[0][at, :] = both
+            put_stat(outs[1], at, lane, lo + h, top, l_both)
+
+    def finish(i, o, total):
         row = lax.broadcasted_iota(jnp.int32, (TM, 128), 0) + i * TM
-        out_ref[at, :] = jnp.where(row < n_ref[1], normed, 0.0).astype(out_ref.dtype)
-
-
-def anchor_call(limits, q, halves, own, out, lo, hi):
+        normed = jnp.where(row < n_ref[0], o / total, 0.0)
+        outs[0][pl.ds(i * TM, TM), :] = normed.astype(outs[0].dtype)
+
+    @pl.when(seen <= 0)
+    def _():
+        for i in range(rows // TM):
+            at = pl.ds(i * TM, TM)
+            if final:
+                finish(i, o_ref[at, :], pick(stat_ref[at, :], lane, lo + h + 64))
+            else:
+                outs[0][at, :] = o_ref[at, :]
+
+    for n in range(1, parts + 1):
+        low = seen > (n - 1) * part
+
+        @pl.when(low & (seen <= n * part) if n < parts else low)
+        def _(n=n):
+            col = lax.broadcasted_iota(jnp.int32, (1, part), 1) + (n - 1) * part
+            bias = jnp.where(col < seen, 0.0, NEG)
+
+            def score(i):
+                q = q_ref[i * TM : (i + 1) * TM, :]
+                parts = [scores(q, k_all[j * part : (j + 1) * part, :]) for j in range(n)]
+                return parts[:-1] + [parts[-1] + bias]
+
+            ready = score(0)
+            for i in range(rows // TM):
+                s_parts = ready
+                if (i + 1) * TM < rows:
+                    ready = score(i + 1)
+                store(i, *attend(s_parts, [v_all[j * part : (j + 1) * part, :] for j in range(n)]))
+
+
+def anchor_call(table, seen_at, q, kv, state, lo, hi, final=False, out=None):
     rows = q.shape[0]
-    n = hi - lo
-    kv = halves[0].shape[1] // (2 * HD)
-    part = halves[0].shape[0] // 2
-    arrays = [halves[0], halves[0], halves[1], halves[1]]
-    k_specs = [pl.BlockSpec((part, HD), lambda h, _, p=p: (p % 2, (lo + h) // GROUP)) for p in range(4)]
-    v_specs = [
-        pl.BlockSpec((part, HD), lambda h, _, p=p: (p % 2, kv + (lo + h) // GROUP)) for p in range(4)
-    ]
-    in_specs = [
-        pl.BlockSpec((rows, HD), lambda h, _: (0, lo + h)),
-        *k_specs,
-        *v_specs,
-        pl.BlockSpec((rows, HD), lambda h, _: (0, h)),
-        pl.BlockSpec((rows, 128), lambda h, _: (0, 0)),
-        pl.BlockSpec(memory_space=pl.ANY),
-    ]
-    operands = [limits, q, *arrays, *arrays, *own, q if out is None else out]
+    n, parts = hi - lo, 2 * len(kv)
+    base = kv[0].shape[1] // (2 * HD)
+    part = kv[0].shape[0] // 2
+    head = pl.BlockSpec((rows, HD), lambda h, _: (0, lo + h))
+    stat = pl.BlockSpec((rows, 128), lambda h, _: (0, 0))
+
+    def block(p, at):
+        return pl.BlockSpec((part, HD), lambda h, _: (p % 2, at + (lo + h) // GROUP))
+
+    in_specs = [head]
+    in_specs += [block(p, 0) for p in range(parts)] + [block(p, base) for p in range(parts)]
+    in_specs += [head, stat]
+    operands = [table, q] + [kv[p // 2] for p in range(parts)] * 2 + list(state)
+    if final:
+        in_specs.append(pl.BlockSpec(memory_space=pl.ANY))
+        operands.append(q if out is None else out)
+        shapes, out_specs = [jax.ShapeDtypeStruct(q.shape, q.dtype)], [head]
+        aliases = {} if out is None else {len(operands) - 1: 0}
+    else:
+        shapes, out_specs = state_shapes(q), [head, stat]
+        aliases = {len(operands) - 2: 0, len(operands) - 1: 1}
     return pl.pallas_call(
-        functools.partial(anchor_kernel, 4),
+        functools.partial(anchor_kernel, lo, parts, seen_at, final),
         grid_spec=pltpu.PrefetchScalarGridSpec(
             num_scalar_prefetch=1,
             grid=(n,),
             in_specs=in_specs,
-            out_specs=pl.BlockSpec((rows, HD), lambda h, _: (0, lo + h)),
+            out_specs=out_specs,
+            scratch_shapes=[
+                pltpu.VMEM((parts * part, HD), q.dtype),
+                pltpu.VMEM((parts * part, 2 * HD), q.dtype),
+            ],
         ),
-        out_shape=jax.ShapeDtypeStruct(q.shape, q.dtype),
-        input_output_aliases={} if out is None else {len(operands) - 1: 0},
+        out_shape=shapes,
+        input_output_aliases=aliases,
         compiler_params=pltpu.CompilerParams(vmem_limit_bytes=WIDE),
         cost_estimate=pl.CostEstimate(
-            flops=n * rows * rows * HD * 12, bytes_accessed=n * rows * HD * 10, transcendentals=0
+            flops=n * rows * rows * HD * 3 * parts,
+            bytes_accessed=n * rows * HD * 10,
+            transcendentals=0,
         ),
         name="anchor",
     )(*operands)
@@ -245,7 +316,7 @@
                 scores(q, k_ref[:, at]) + bias,
                 jnp.where(seen, scores(q, k2_ref[0, :, at]), NEG),
             ]
-            m, total, o = attend(s_parts, [v_ref[:, at], v2_ref[0, :, at]])
+            m, total, o = attend(s_parts, [wide(v_ref[:, at]), wide(v2_ref[0, :, at])])
             o = o / total
             if i == 0:
                 outs[0][:, cols] = o
@@ -253,7 +324,7 @@
                 sent_ref[:, cols] = o.astype(sent_ref.dtype)
             tops = jnp.where(lane == h, m, tops)
             totals = jnp.where(lane == h, total, totals)
-        lse = tops * C + jnp.log2(totals)
+        lse = tops + jnp.log2(totals)
         if i == 0:
             outs[1][...] = lse
         else:
@@ -353,6 +424,15 @@
         ),
         name="project",
     )(limits, w, mine, theirs)
+
+
+def runs(total, shares):
+    whole, at, out = sum(shares), 0, []
+    for i in range(len(shares)):
+        end = total * sum(shares[: i + 1]) // whole
+        out.append((at, end))
+        at = end
+    return out
 
 
 def per_device(
@@ -380,63 +460,78 @@
     def side_of(step):
         return (my_code >> grid.bit(step, odd)) & 1
 
-    def far(root, step):
+    def is_far(root, step):
         return ((code_of(root) ^ my_code) >> grid.bit(step, odd)) & 1 == 1
 
     def hop(x, step):
         return grid.hop(x, step)
 
-    def cut(x, side):
-        half = x.shape[0] // 2
-        return lax.dynamic_slice_in_dim(x, side * half, half, 0)
+    def cut(x, first):
+        sizes = (x.shape[0] // 2, x.shape[1])
+        zero = jnp.zeros((), first.dtype)
+        return lax.dynamic_slice(x, (first, zero), sizes, allow_negative_indices=False)
+
+    side, side1 = side_of(0), side_of(1)
+    query = query_q[0]
+    got = hop(cut(query, (1 - side) * (query.shape[0] // 2)), 0)
+
+    q_rows, part = query.shape[0] // 2, rows // 4
+    places = [part * side1, part * (1 - side1)]
+    in_view = jnp.where(me == anchor, 0, counts[anchor])
+    table = jnp.stack(
+        [
+            counts[me],
+            (me == owner).astype(jnp.int32),
+            side * q_rows,
+            (1 - side) * q_rows,
+            in_view - 2 * part * side,
+            *places,
+            in_view - 2 * part * (1 - side),
+            *places,
+            in_view,
+            *[2 * part * s0 + x for s0 in (side, 1 - side) for x in places],
+        ]
+    )
+    q_far = [is_far(owner, step) for step in range(grid.dims)]
+    a_far = [is_far(anchor, step) for step in range(grid.dims)]
+    half = rows // 2
+    firsts = [side * q_rows, side * half, (1 - side) * half, side1 * part, (1 - side1) * part]
+    firsts, table, q_far, a_far, odd, query, ctx_q, ctx_k, ctx_v = lax.optimization_barrier(
+        (firsts, table, q_far, a_far, odd, query, ctx_q, ctx_k, ctx_v)
+    )
 
     last = grid.dims - 1
-    side = side_of(0)
-    query = query_q[0]
-    q_rows = query.shape[0] // 2
-    qa = jnp.where(far(owner, 0), hop(cut(query, 1 - side), 0), cut(query, side))
+    qa = jnp.where(q_far[0], got, cut(query, firsts[0]))
     for step in range(1, grid.dims):
-        qa = jnp.where(far(owner, step), hop(qa, step), qa)
+        qa = jnp.where(q_far[step], hop(qa, step), qa)
     qb = hop(qa, 0)
-
-    side1 = side_of(1)
 
     def both(cutter):
         return jnp.concatenate([cutter(ctx_k), cutter(ctx_v)], axis=1)
 
     mine = jnp.where(
-        far(anchor, 0),
-        hop(both(lambda x: cut(x, 1 - side)), 0),
-        both(lambda x: cut(x, side)),
-    )
-    mine = jnp.where(far(anchor, 1), hop(cut(mine, 1 - side1), 1), cut(mine, side1))
+        a_far[0],
+        hop(both(lambda x: cut(x, firsts[2])), 0),
+        both(lambda x: cut(x, firsts[1])),
+    )
+    mine = jnp.where(a_far[1], hop(cut(mine, firsts[4]), 1), cut(mine, firsts[3]))
     for step in range(2, grid.dims):
-        mine = jnp.where(far(anchor, step), hop(mine, step), mine)
+        mine = jnp.where(a_far[step], hop(mine, step), mine)
     mine = jnp.concatenate([mine, hop(mine, 1)], axis=0)
     halves = [mine, hop(mine, 0)]
-    part = rows // 4
-    starts = [
-        2 * part * s0 + part * s1 for s0 in (side, 1 - side) for s1 in (side1, 1 - side1)
-    ]
-
-    pieces = 4
-    width = heads // pieces
-    cuts = [(i * width, (i + 1) * width) for i in range(pieces)]
-    own = []
-    for a, b in cuts:
-        own.append(own_call(ctx_q, ctx_k, ctx_v, a, b))
-
-    q_limits = jnp.stack(
-        [counts[me], (me == owner).astype(jnp.int32), side * q_rows, (1 - side) * q_rows]
-    )
-    o, lse, sent = query_call(q_limits, qa, qb, ctx_k, ctx_v, query_k, query_v)
+
+    state = None
+    for a, b in runs(heads, (2, 2, 2, 2)):
+        state = own_call(ctx_q, ctx_k, ctx_v, state, a, b)
+
+    o, lse, sent = query_call(table, qa, qb, ctx_k, ctx_v, query_k, query_v)
     for step in range(grid.dims):
         got = hop(sent, step)
         done = merge_call(o, lse, got, step == last)
         if step < last:
             o, lse, sent = done
     theirs = hop(done[0], 0)
-    partial = project_call(q_limits, done[0], theirs, out_weight)
+    partial = project_call(table, done[0], theirs, out_weight)
 
     top = partial.shape[0] // 2
     low, high = partial[:top], partial[top:]
@@ -453,10 +548,14 @@
         odd, jnp.concatenate([rest, ours], axis=0), jnp.concatenate([ours, rest], axis=0)
     )
 
-    limits = jnp.stack([jnp.where(me == anchor, 0, counts[anchor]), counts[me], *starts])
+    cuts = runs(heads, (2, 2, 2, 2))
+    state = anchor_call(table, 4, ctx_q, halves[:1], state, *cuts[0])
     out = None
-    for i, (a, b) in enumerate(cuts):
-        out = anchor_call(limits, ctx_q, halves, own[i], out, a, b)
+    for a, b in cuts[1:]:
+        (out,) = anchor_call(table, 10, ctx_q, halves, state, a, b, final=True, out=out)
+    (out,) = anchor_call(
+        table, 7, ctx_q, halves[1:], state, *cuts[0], final=True, out=out
+    )
     return out, answer
 
 

time: 114 us -> 103 us (0.904)
  Pallas kernels: 57.6 us -> 36.2 us
  waiting for transfers between devices: 20.1 us -> 28.6 us
  starting transfers between devices: 24.5 us -> 28 us
  other arithmetic: 3.88 us -> 2.34 us
    pallas_call x8 -> x9, Pallas kernels: 50.7 us -> 29.6 us  [the longest x5 18.1 us: anchor_call(): pl.pallas_call(functools.partial(anchor_kernel, lo, parts, seen_at, final...]
    ppermute x13, waiting for transfers between devices: 20.1 us -> 28.4 us  [hop(): return lax.ppermute(value, ('blk', 'head'), pairs)]
    ppermute x13, starting transfers between devices: 22.5 us -> 26.2 us  [hop(): return lax.ppermute(value, ('blk', 'head'), pairs)]
  transfers between devices with their start and end apart: 16 -> 16, of which waited for: 5 -> 9; matrix products, arithmetic and copies ran while one was open for 5% -> 5% of each run, Pallas kernels for 50% -> 34%
where the time goes in v1:
time: 103 us
  Pallas kernels  36.2 us (35%)
  waiting for transfers between devices  28.6 us (28%)
  starting transfers between devices  28 us (27%)
  local copies, waits for them, and re-layouts  4.73 us (5%)
  between operations  2.91 us (3%)
  other arithmetic  2.34 us (2%)
    ppermute x13, waiting for transfers between devices, hop(): return lax.ppermute(value, ('blk', 'head'), pairs)  28.4 us
    ppermute x13, starting transfers between devices, hop(): return lax.ppermute(value, ('blk', 'head'), pairs)  26.2 us
    pallas_call x5, Pallas kernels, anchor_call(): pl.pallas_call(functools.partial(anchor_kernel, lo, parts, seen_at, final...  18.1 us
    pallas_call x4, Pallas kernels, own_call(): pl.pallas_call(functools.partial(own_kernel, lo), grid=(n,), in_specs=[he...  11.5 us
    pallas_call x1, Pallas kernels, query_call(): pl.pallas_call(kernel, in_specs=[pl.BlockSpec(memory_space=pltpu.SMEM)] +...  4.25 us
    dynamic_slice x3, local copies, waits for them, and re-layouts, cut(): lax.dynamic_slice(x, (first, zero), sizes, allow_negative_indices=False)  2.58 us
  transfers between devices with their start and end apart: 16, of which 9 were waited for; matrix products, arithmetic and copies ran while one was open for 5% of the time, Pallas kernels for 34%

profile of v1, /device:TPU:0, one launch (start us, length us, event | category | flops | bytes accessed | tf_op | source)
XLA Modules:
  0.0 102.8 jit_solution(13315278700388776951)
XLA Ops:
  1.6 3.0 %collective-permute-start.5 = (bf16[128,1024]{1,0:T(8,128)(2,1)S(1)}, bf16[128,1024]{1,0:T(8,128)(2,1)S(1)}, u32[]{:S(2)}, u32[]{:S(2)}) collective-permute-start(bf16[128,1024]{1,0:T(8,128)(2,1)S(1)} %dynamic-slice_bitcast_fusion), channel_id=1, source_target_pairs={{0,4},{1,9},{2,6},{3,11},{4,0},{5,13},{6,2},{7,15},{8,12},{9,1},{1... | collective-permute-start | bytes 786440 | tf_op jit(solution)/shard_map/ppermute | solution.py:58
  11.6 2.1 %collective-permute-start.6 = (bf16[128,1024]{1,0:T(8,128)(2,1)S(1)}, bf16[128,1024]{1,0:T(8,128)(2,1)S(1)}, u32[]{:S(2)}, u32[]{:S(2)}) collective-permute-start(bf16[128,1024]{1,0:T(8,128)(2,1)S(1)} %dynamic-slice_select_fusion), channel_id=1, source_target_pairs={{0,8},{1,25},{2,10},{3,27},{4,12},{5,29},{6,14},{7,31},{8,0},{9,17... | collective-permute-start | bytes 786440 | tf_op jit(solution)/shard_map/ppermute | solution.py:58
  13.7 7.2 %collective-permute-done.6 = bf16[128,1024]{1,0:T(8,128)(2,1)S(1)} collective-permute-done((bf16[128,1024]{1,0:T(8,128)(2,1)S(1)}, bf16[128,1024]{1,0:T(8,128)(2,1)S(1)}, u32[]{:S(2)}, u32[]{:S(2)}) %collective-permute-start.6) | collective-permute-done | bytes 262176 | tf_op jit(solution)/shard_map/ppermute | solution.py:58
  20.9 5.6 %collective-permute-start.7 = (bf16[128,1024]{1,0:T(8,128)(2,1)S(1)}, bf16[128,1024]{1,0:T(8,128)(2,1)S(1)}, u32[]{:S(2)}, u32[]{:S(2)}) collective-permute-start(bf16[128,1024]{1,0:T(8,128)(2,1)S(1)} %broadcast_select_fusion), channel_id=1, source_target_pairs={{0,24},{1,5},{2,26},{3,7},{4,28},{5,1},{6,30},{7,3},{8,16},{9,13},... | collective-permute-start | bytes 786440 | tf_op jit(solution)/shard_map/ppermute | solution.py:58
  26.8 6.2 %collective-permute-done.7 = bf16[128,1024]{1,0:T(8,128)(2,1)S(1)} collective-permute-done((bf16[128,1024]{1,0:T(8,128)(2,1)S(1)}, bf16[128,1024]{1,0:T(8,128)(2,1)S(1)}, u32[]{:S(2)}, u32[]{:S(2)}) %collective-permute-start.7) | collective-permute-done | bytes 262176 | tf_op jit(solution)/shard_map/ppermute | solution.py:58
  33.0 1.7 %collective-permute-start.8 = (bf16[128,1024]{1,0:T(8,128)(2,1)S(1)}, bf16[128,1024]{1,0:T(8,128)(2,1)S(1)}, u32[]{:S(2)}, u32[]{:S(2)}) collective-permute-start(bf16[128,1024]{1,0:T(8,128)(2,1)S(1)} %broadcast_select_fusion.1.refs_1_), channel_id=1, source_target_pairs={{0,4},{1,9},{2,6},{3,11},{4,0},{5,13},{6,2},{7,15},{8,12},{9,1},{1... | collective-permute-start | bytes 786440 | tf_op jit(solution)/shard_map/ppermute | solution.py:58
  34.8 3.9 %collective-permute-done.1 = bf16[256,512]{1,0:T(8,128)(2,1)S(1)} collective-permute-done((bf16[256,512]{1,0:T(8,128)(2,1)S(1)}, bf16[256,512]{1,0:T(8,128)(2,1)S(1)}, u32[]{:S(2)}, u32[]{:S(2)}) %collective-permute-start.1) | collective-permute-done | bytes 262176 | tf_op jit(solution)/shard_map/ppermute | solution.py:58
  40.3 4.2 %query.1 = (f32[128,1024]{1,0:T(8,128)S(1)}, f32[128,128]{1,0:T(8,128)S(1)}, bf16[128,1152]{1,0:T(8,128)(2,1)S(1)}) custom-call(s32[15]{0:T(128)S(1)} %stack.57.n_ref.refs_0_, bf16[128,1024]{1,0:T(8,128)(2,1)S(1)} %broadcast_select_fusion.1.refs_1_, bf16[128,1024]{1,0:T(8,128)(2,1)S(1)} %collective-permute-done.8.refs_2_, bf16[1024,256]{1,0:T(8,128)(2,1)S(1)} %copy-done.3, ...), custom_call_target="tpu_custom_call" | custom-call | flops 2415919104 | bytes 1048576 | tf_op jit(solution)/shard_map/query/pallas_call | solution.py:349
  44.5 2.2 %collective-permute-start.9 = (bf16[128,1152]{1,0:T(8,128)(2,1)S(1)}, bf16[128,1152]{1,0:T(8,128)(2,1)S(1)}, u32[]{:S(2)}, u32[]{:S(2)}) collective-permute-start(bf16[128,1152]{1,0:T(8,128)(2,1)S(1)} %get-tuple-element.67), channel_id=1, source_target_pairs={{0,4},{1,9},{2,6},{3,11},{4,0},{5,13},{6,2},{7,15},{8,12},{9,1},{1... | collective-permute-start | bytes 884744 | tf_op jit(solution)/shard_map/ppermute | solution.py:58
  47.2 8.1 %collective-permute-start.3 = (bf16[256,512]{1,0:T(8,128)(2,1)S(1)}, bf16[256,512]{1,0:T(8,128)(2,1)S(1)}, u32[]{:S(2)}, u32[]{:S(2)}) collective-permute-start(bf16[256,512]{1,0:T(8,128)(2,1)S(1)} %broadcast_select_fusion.2), channel_id=1, source_target_pairs={{0,8},{1,25},{2,10},{3,27},{4,12},{5,29},{6,14},{7,31},{8,0},{9,17... | collective-permute-start | bytes 786440 | tf_op jit(solution)/shard_map/ppermute | solution.py:58
  55.3 2.8 %own.4 = (f32[1024,1024]{1,0:T(8,128)S(1)}, f32[1024,128]{1,0:T(8,128)S(1)}) custom-call(bf16[1024,1024]{1,0:T(8,128)(2,1)S(1)} %copy-done, bf16[1024,256]{1,0:T(8,128)(2,1)S(1)} %copy-done.3, bf16[1024,256]{1,0:T(8,128)(2,1)S(1)} %copy-done.2), custom_call_target="tpu_custom_call" | custom-call | flops 2147483648 | bytes 2621440 | tf_op jit(solution)/shard_map/own/pallas_call | solution.py:145
  58.1 2.9 %own.5 = (f32[1024,1024]{1,0:T(8,128)S(1)}, f32[1024,128]{1,0:T(8,128)S(1)}) custom-call(bf16[1024,1024]{1,0:T(8,128)(2,1)S(1)} %copy-done, bf16[1024,256]{1,0:T(8,128)(2,1)S(1)} %copy-done.3, bf16[1024,256]{1,0:T(8,128)(2,1)S(1)} %copy-done.2, f32[1024,1024]{1,0:T(8,128)S(1)} %get-tuple-element.49.refs_0_, ...), custom_call_target="tpu_custom_call", output_to_operand_aliasing={{0}: (3, {}), {1}: (4, {})} | custom-call | flops 2147483648 | bytes 2621440 | tf_op jit(solution)/shard_map/own/pallas_call | solution.py:145
  61.8 3.6 %collective-permute-done.3 = bf16[256,512]{1,0:T(8,128)(2,1)S(1)} collective-permute-done((bf16[256,512]{1,0:T(8,128)(2,1)S(1)}, bf16[256,512]{1,0:T(8,128)(2,1)S(1)}, u32[]{:S(2)}, u32[]{:S(2)}) %collective-permute-start.3) | collective-permute-done | bytes 262176 | tf_op jit(solution)/shard_map/ppermute | solution.py:58
  65.7 2.9 %own.6 = (f32[1024,1024]{1,0:T(8,128)S(1)}, f32[1024,128]{1,0:T(8,128)S(1)}) custom-call(bf16[1024,1024]{1,0:T(8,128)(2,1)S(1)} %copy-done, bf16[1024,256]{1,0:T(8,128)(2,1)S(1)} %copy-done.3, bf16[1024,256]{1,0:T(8,128)(2,1)S(1)} %copy-done.2, f32[1024,1024]{1,0:T(8,128)S(1)} %get-tuple-element.51.refs_0_, ...), custom_call_target="tpu_custom_call", output_to_operand_aliasing={{0}: (3, {}), {1}: (4, {})} | custom-call | flops 2147483648 | bytes 2621440 | tf_op jit(solution)/shard_map/own/pallas_call | solution.py:145
  68.6 2.9 %collective-permute-done.10.got_ref = bf16[128,1152]{1,0:T(8,128)(2,1)S(1)} collective-permute-done((bf16[128,1152]{1,0:T(8,128)(2,1)S(1)}, bf16[128,1152]{1,0:T(8,128)(2,1)S(1)}, u32[]{:S(2)}, u32[]{:S(2)}) %collective-permute-start.10) | collective-permute-done | bytes 294944 | tf_op jit(solution)/shard_map/ppermute | solution.py:58
  72.5 2.9 %own.7 = (f32[1024,1024]{1,0:T(8,128)S(1)}, f32[1024,128]{1,0:T(8,128)S(1)}) custom-call(bf16[1024,1024]{1,0:T(8,128)(2,1)S(1)} %copy-done, bf16[1024,256]{1,0:T(8,128)(2,1)S(1)} %copy-done.3, bf16[1024,256]{1,0:T(8,128)(2,1)S(1)} %copy-done.2, f32[1024,1024]{1,0:T(8,128)S(1)} %get-tuple-element.53.refs_0_, ...), custom_call_target="tpu_custom_call", output_to_operand_aliasing={{0}: (3, {}), {1}: (4, {})} | custom-call | flops 2147483648 | bytes 2621440 | tf_op jit(solution)/shard_map/own/pallas_call | solution.py:145
  75.4 3.4 %anchor.5 = (f32[1024,1024]{1,0:T(8,128)S(1)}, f32[1024,128]{1,0:T(8,128)S(1)}) custom-call(s32[15]{0:T(128)S(1)} %stack.57.n_ref.refs_0_, bf16[1024,1024]{1,0:T(8,128)(2,1)S(1)} %copy-done, bf16[512,512]{1,0:T(8,128)(2,1)S(1)} %pad_maximum_fusion.1.refs_0_.refs_1_.refs_2_.refs_3_.refs_4_.refs_5_, ...), custom_call_target="tpu_custom_call", output_to_operand_aliasing={{0}: (6, {}), {1}: (7, {})} | custom-call | flops 1610612736 | bytes 2621440 | tf_op jit(solution)/shard_map/anchor/pallas_call | solution.py:258
  78.8 2.8 %collective-permute-done.11.got_ref = bf16[128,1152]{1,0:T(8,128)(2,1)S(1)} collective-permute-done((bf16[128,1152]{1,0:T(8,128)(2,1)S(1)}, bf16[128,1152]{1,0:T(8,128)(2,1)S(1)}, u32[]{:S(2)}, u32[]{:S(2)}) %collective-permute-start.11) | collective-permute-done | bytes 294944 | tf_op jit(solution)/shard_map/ppermute | solution.py:58
  82.7 4.2 %anchor.6.refs_10_ = bf16[1024,1024]{1,0:T(8,128)(2,1)} custom-call(s32[15]{0:T(128)S(1)} %stack.57.n_ref.refs_0_, bf16[1024,1024]{1,0:T(8,128)(2,1)S(1)} %copy-done, bf16[512,512]{1,0:T(8,128)(2,1)S(1)} %pad_maximum_fusion.1.refs_0_.refs_1_.refs_2_.refs_3_.refs_4_.refs_5_, ...), custom_call_target="tpu_custom_call" | custom-call | flops 3221225472 | bytes 2621440 | tf_op jit(solution)/shard_map/anchor/pallas_call | solution.py:258
  86.9 1.5 %collective-permute-done.12.theirs_ref = bf16[128,1024]{1,0:T(8,128)(2,1)S(1)} collective-permute-done((bf16[128,1024]{1,0:T(8,128)(2,1)S(1)}, bf16[128,1024]{1,0:T(8,128)(2,1)S(1)}, u32[]{:S(2)}, u32[]{:S(2)}) %collective-permute-start.12) | collective-permute-done | bytes 262176 | tf_op jit(solution)/shard_map/ppermute | solution.py:58
  89.6 4.0 %anchor.7.refs_10_ = bf16[1024,1024]{1,0:T(8,128)(2,1)} custom-call(s32[15]{0:T(128)S(1)} %stack.57.n_ref.refs_0_, bf16[1024,1024]{1,0:T(8,128)(2,1)S(1)} %copy-done, bf16[512,512]{1,0:T(8,128)(2,1)S(1)} %pad_maximum_fusion.1.refs_0_.refs_1_.refs_2_.refs_3_.refs_4_.refs_5_, ...), custom_call_target="tpu_custom_call", output_to_operand_aliasing={{}: (12, {})} | custom-call | flops 3221225472 | bytes 2621440 | tf_op jit(solution)/shard_map/anchor/pallas_call | solution.py:258
  93.6 1.6 %collective-permute-start.14 = (bf16[128,512]{1,0:T(8,128)(2,1)S(1)}, bf16[128,512]{1,0:T(8,128)(2,1)S(1)}, u32[]{:S(2)}, u32[]{:S(2)}) collective-permute-start(bf16[128,512]{1,0:T(8,128)(2,1)S(1)} %add_convert_fusion.1), channel_id=1, source_target_pairs={{0,2},{1,3},{2,0},{3,1},{4,6},{5,7},{6,4},{7,5},{8,10},{9,11},{10,... | collective-permute-start | bytes 393224 | tf_op jit(solution)/shard_map/ppermute | solution.py:61
  95.2 4.2 %anchor.8.refs_6_ = bf16[1024,1024]{1,0:T(8,128)(2,1)} custom-call(s32[15]{0:T(128)S(1)} %stack.57.n_ref.refs_0_, bf16[1024,1024]{1,0:T(8,128)(2,1)S(1)} %copy-done, bf16[512,512]{1,0:T(8,128)(2,1)S(1)} %pad_maximum_fusion.1.refs_0_.refs_1_.refs_2_.refs_3_.refs_4_.refs_5_, ...), custom_call_target="tpu_custom_call", output_to_operand_aliasing={{}: (12, {})} | custom-call | flops 3221225472 | bytes 2621440 | tf_op jit(solution)/shard_map/anchor/pallas_call | solution.py:258
  99.8 2.2 %anchor.9 = bf16[1024,1024]{1,0:T(8,128)(2,1)} custom-call(s32[15]{0:T(128)S(1)} %stack.57.n_ref.refs_0_, bf16[1024,1024]{1,0:T(8,128)(2,1)S(1)} %copy-done, bf16[512,512]{1,0:T(8,128)(2,1)S(1)} %collective-permute-done.4.refs_2_.refs_3_.refs_6_.refs_7_.refs_0_.refs_1_, ...), custom_call_target="tpu_custom_call", output_to_operand_aliasing={{}: (8, {})} | custom-call | flops 1610612736 | bytes 2621440 | tf_op jit(solution)/shard_map/anchor/pallas_call | solution.py:258
  (51 shorter events, 13.6 us)
Async XLA Ops:
  1.6 8.9 %collective-permute-start.5 = (bf16[128,1024]{1,0:T(8,128)(2,1)S(1)}, bf16[128,1024]{1,0:T(8,128)(2,1)S(1)}, u32[]{:S(2)}, u32[]{:S(2)}) collective-permute-start(bf16[128,1024]{1,0:T(8,128)(2,1)S(1)} %dynamic-slice_bitcast_fusion), channel_id=1, source_target_pairs={{0,4},{1,9},{2,6},{3,11},{4,0},{5,13},{6,2},{7,15},{8,12},{9,1},{1... | collective-permute-start | bytes 786440 | tf_op jit(solution)/shard_map/ppermute | solution.py:58
  8.8 31.4 %copy-start.2 = (bf16[1024,256]{1,0:T(8,128)(2,1)S(1)}, bf16[1024,256]{1,0:T(8,128)(2,1)}, u32[]{:S(2)}) copy-start(bf16[1024,256]{1,0:T(8,128)(2,1)} %refs_4_) | copy-start | bytes 1572868
  8.8 31.4 %copy-start.3 = (bf16[1024,256]{1,0:T(8,128)(2,1)S(1)}, bf16[1024,256]{1,0:T(8,128)(2,1)}, u32[]{:S(2)}) copy-start(bf16[1024,256]{1,0:T(8,128)(2,1)} %refs_3_) | copy-start | bytes 1572868
  8.8 31.4 %copy-start.4 = (bf16[1,256,256]{2,1,0:T(8,128)(2,1)S(1)}, bf16[1,256,256]{2,1,0:T(8,128)(2,1)}, u32[]{:S(2)}) copy-start(bf16[1,256,256]{2,1,0:T(8,128)(2,1)} %refs_5_.1) | copy-start | bytes 393220
  8.8 31.4 %copy-start.5 = (bf16[1,256,256]{2,1,0:T(8,128)(2,1)S(1)}, bf16[1,256,256]{2,1,0:T(8,128)(2,1)}, u32[]{:S(2)}) copy-start(bf16[1,256,256]{2,1,0:T(8,128)(2,1)} %refs_6_.1) | copy-start | bytes 393220
  10.4 16.1 %collective-permute-start = (bf16[512,512]{1,0:T(8,128)(2,1)S(1)}, bf16[512,512]{1,0:T(8,128)(2,1)S(1)}, u32[]{:S(2)}, u32[]{:S(2)}) collective-permute-start(bf16[512,512]{1,0:T(8,128)(2,1)S(1)} %pad_maximum_fusion), channel_id=1, source_target_pairs={{0,4},{1,9},{2,6},{3,11},{4,0},{5,13},{6,2},{7,15},{8,12},{9,1},{1... | collective-permute-start | bytes 1572872 | tf_op jit(solution)/shard_map/ppermute | solution.py:58
  11.6 9.3 %collective-permute-start.6 = (bf16[128,1024]{1,0:T(8,128)(2,1)S(1)}, bf16[128,1024]{1,0:T(8,128)(2,1)S(1)}, u32[]{:S(2)}, u32[]{:S(2)}) collective-permute-start(bf16[128,1024]{1,0:T(8,128)(2,1)S(1)} %dynamic-slice_select_fusion), channel_id=1, source_target_pairs={{0,8},{1,25},{2,10},{3,27},{4,12},{5,29},{6,14},{7,31},{8,0},{9,17... | collective-permute-start | bytes 786440 | tf_op jit(solution)/shard_map/ppermute | solution.py:58
  20.9 12.1 %collective-permute-start.7 = (bf16[128,1024]{1,0:T(8,128)(2,1)S(1)}, bf16[128,1024]{1,0:T(8,128)(2,1)S(1)}, u32[]{:S(2)}, u32[]{:S(2)}) collective-permute-start(bf16[128,1024]{1,0:T(8,128)(2,1)S(1)} %broadcast_select_fusion), channel_id=1, source_target_pairs={{0,24},{1,5},{2,26},{3,7},{4,28},{5,1},{6,30},{7,3},{8,16},{9,13},... | collective-permute-start | bytes 786440 | tf_op jit(solution)/shard_map/ppermute | solution.py:58
  26.7 11.9 %collective-permute-start.1 = (bf16[256,512]{1,0:T(8,128)(2,1)S(1)}, bf16[256,512]{1,0:T(8,128)(2,1)S(1)}, u32[]{:S(2)}, u32[]{:S(2)}) collective-permute-start(bf16[256,512]{1,0:T(8,128)(2,1)S(1)} %constant_dynamic-slice_fusion), channel_id=1, source_target_pairs={{0,8},{1,25},{2,10},{3,27},{4,12},{5,29},{6,14},{7,31},{8,0},{9,17... | collective-permute-start | bytes 786440 | tf_op jit(solution)/shard_map/ppermute | solution.py:58
  33.0 7.2 %collective-permute-start.8 = (bf16[128,1024]{1,0:T(8,128)(2,1)S(1)}, bf16[128,1024]{1,0:T(8,128)(2,1)S(1)}, u32[]{:S(2)}, u32[]{:S(2)}) collective-permute-start(bf16[128,1024]{1,0:T(8,128)(2,1)S(1)} %broadcast_select_fusion.1.refs_1_), channel_id=1, source_target_pairs={{0,4},{1,9},{2,6},{3,11},{4,0},{5,13},{6,2},{7,15},{8,12},{9,1},{1... | collective-permute-start | bytes 786440 | tf_op jit(solution)/shard_map/ppermute | solution.py:58
  38.7 16.6 %copy-start = (bf16[1024,1024]{1,0:T(8,128)(2,1)S(1)}, bf16[1024,1024]{1,0:T(8,128)(2,1)}, u32[]{:S(2)}) copy-start(bf16[1024,1024]{1,0:T(8,128)(2,1)} %q_ref.8) | copy-start | bytes 6291460
  38.7 8.4 %collective-permute-start.2 = (bf16[256,512]{1,0:T(8,128)(2,1)S(1)}, bf16[256,512]{1,0:T(8,128)(2,1)S(1)}, u32[]{:S(2)}, u32[]{:S(2)}) collective-permute-start(bf16[256,512]{1,0:T(8,128)(2,1)S(1)} %dynamic-slice_select_fusion.1), channel_id=1, source_target_pairs={{0,24},{1,5},{2,26},{3,7},{4,28},{5,1},{6,30},{7,3},{8,16},{9,13},... | collective-permute-start | bytes 786440 | tf_op jit(solution)/shard_map/ppermute | solution.py:58
  44.5 16.6 %collective-permute-start.9 = (bf16[128,1152]{1,0:T(8,128)(2,1)S(1)}, bf16[128,1152]{1,0:T(8,128)(2,1)S(1)}, u32[]{:S(2)}, u32[]{:S(2)}) collective-permute-start(bf16[128,1152]{1,0:T(8,128)(2,1)S(1)} %get-tuple-element.67), channel_id=1, source_target_pairs={{0,4},{1,9},{2,6},{3,11},{4,0},{5,13},{6,2},{7,15},{8,12},{9,1},{1... | collective-permute-start | bytes 884744 | tf_op jit(solution)/shard_map/ppermute | solution.py:58
  47.2 18.3 %collective-permute-start.3 = (bf16[256,512]{1,0:T(8,128)(2,1)S(1)}, bf16[256,512]{1,0:T(8,128)(2,1)S(1)}, u32[]{:S(2)}, u32[]{:S(2)}) collective-permute-start(bf16[256,512]{1,0:T(8,128)(2,1)S(1)} %broadcast_select_fusion.2), channel_id=1, source_target_pairs={{0,8},{1,25},{2,10},{3,27},{4,12},{5,29},{6,14},{7,31},{8,0},{9,17... | collective-permute-start | bytes 786440 | tf_op jit(solution)/shard_map/ppermute | solution.py:58
  61.5 10.0 %collective-permute-start.10 = (bf16[128,1152]{1,0:T(8,128)(2,1)S(1)}, bf16[128,1152]{1,0:T(8,128)(2,1)S(1)}, u32[]{:S(2)}, u32[]{:S(2)}) collective-permute-start(bf16[128,1152]{1,0:T(8,128)(2,1)S(1)} %get-tuple-element.70), channel_id=1, source_target_pairs={{0,8},{1,25},{2,10},{3,27},{4,12},{5,29},{6,14},{7,31},{8,0},{9,17... | collective-permute-start | bytes 884744 | tf_op jit(solution)/shard_map/ppermute | solution.py:58
  65.5 17.2 %collective-permute-start.4 = (bf16[512,512]{1,0:T(8,128)(2,1)S(1)}, bf16[512,512]{1,0:T(8,128)(2,1)S(1)}, u32[]{:S(2)}, u32[]{:S(2)}) collective-permute-start(bf16[512,512]{1,0:T(8,128)(2,1)S(1)} %pad_maximum_fusion.1.refs_0_.refs_1_.refs_2_.refs_3_.refs_4_.refs_5_), channel_id=1, source_target_pairs={{0,4},{1,9},{2,6},{3,11},{4,0},{5,13},{6,2},{7,15},{8,12},{9,1},{1... | collective-permute-start | bytes 1572872 | tf_op jit(solution)/shard_map/ppermute | solution.py:58
  72.0 9.6 %collective-permute-start.11 = (bf16[128,1152]{1,0:T(8,128)(2,1)S(1)}, bf16[128,1152]{1,0:T(8,128)(2,1)S(1)}, u32[]{:S(2)}, u32[]{:S(2)}) collective-permute-start(bf16[128,1152]{1,0:T(8,128)(2,1)S(1)} %get-tuple-element.73), channel_id=1, source_target_pairs={{0,24},{1,5},{2,26},{3,7},{4,28},{5,1},{6,30},{7,3},{8,16},{9,13},... | collective-permute-start | bytes 884744 | tf_op jit(solution)/shard_map/ppermute | solution.py:58
  82.0 6.4 %collective-permute-start.12 = (bf16[128,1024]{1,0:T(8,128)(2,1)S(1)}, bf16[128,1024]{1,0:T(8,128)(2,1)S(1)}, u32[]{:S(2)}, u32[]{:S(2)}) collective-permute-start(bf16[128,1024]{1,0:T(8,128)(2,1)S(1)} %merge.5.mine_ref), channel_id=1, source_target_pairs={{0,4},{1,9},{2,6},{3,11},{4,0},{5,13},{6,2},{7,15},{8,12},{9,1},{1... | collective-permute-start | bytes 786440 | tf_op jit(solution)/shard_map/ppermute | solution.py:58
  82.7 5.8 %copy-start.1 = (bf16[1024,512]{1,0:T(8,128)(2,1)S(1)}, bf16[1024,512]{1,0:T(8,128)(2,1)}, u32[]{:S(2)}) copy-start(bf16[1024,512]{1,0:T(8,128)(2,1)} %w_ref.1) | copy-start | bytes 3145732
  89.5 4.1 %collective-permute-start.13 = (f32[128,512]{1,0:T(8,128)S(1)}, f32[128,512]{1,0:T(8,128)S(1)}, u32[]{:S(2)}, u32[]{:S(2)}) collective-permute-start(f32[128,512]{1,0:T(8,128)S(1)} %slice_select_fusion), channel_id=1, source_target_pairs={{0,1},{1,0},{2,3},{3,2},{4,5},{5,4},{6,7},{7,6},{8,9},{9,8},{10,11... | collective-permute-start | bytes 786440 | tf_op jit(solution)/shard_map/ppermute | solution.py:61
  93.6 6.0 %collective-permute-start.14 = (bf16[128,512]{1,0:T(8,128)(2,1)S(1)}, bf16[128,512]{1,0:T(8,128)(2,1)S(1)}, u32[]{:S(2)}, u32[]{:S(2)}) collective-permute-start(bf16[128,512]{1,0:T(8,128)(2,1)S(1)} %add_convert_fusion.1), channel_id=1, source_target_pairs={{0,2},{1,3},{2,0},{3,1},{4,6},{5,7},{6,4},{7,5},{8,10},{9,11},{10,... | collective-permute-start | bytes 393224 | tf_op jit(solution)/shard_map/ppermute | solution.py:61
  99.6 2.4 %collective-permute-start.15 = (bf16[128,512]{1,0:T(8,128)(2,1)S(1)}, bf16[128,512]{1,0:T(8,128)(2,1)S(1)}, u32[]{:S(2)}, u32[]{:S(2)}) collective-permute-start(bf16[128,512]{1,0:T(8,128)(2,1)S(1)} %add_convert_fusion), channel_id=1, source_target_pairs={{0,1},{1,0},{2,3},{3,2},{4,5},{5,4},{6,7},{7,6},{8,9},{9,8},{10,11... | collective-permute-start | bytes 393224 | tf_op jit(solution)/shard_map/ppermute | solution.py:61

commit v2 on v1

--- a/solution.py
+++ b/solution.py
@@ -548,14 +548,16 @@
         odd, jnp.concatenate([rest, ours], axis=0), jnp.concatenate([ours, rest], axis=0)
     )
 
-    cuts = runs(heads, (2, 2, 2, 2))
-    state = anchor_call(table, 4, ctx_q, halves[:1], state, *cuts[0])
+    cuts = runs(heads, (2, 2, 3, 1))
+    early = (cuts[0][0], cuts[1][1])
+    state = anchor_call(table, 4, ctx_q, halves[:1], state, *early)
     out = None
-    for a, b in cuts[1:]:
+    for a, b in cuts[2:]:
         (out,) = anchor_call(table, 10, ctx_q, halves, state, a, b, final=True, out=out)
-    (out,) = anchor_call(
-        table, 7, ctx_q, halves[1:], state, *cuts[0], final=True, out=out
-    )
+    for a, b in cuts[:2]:
+        (out,) = anchor_call(
+            table, 7, ctx_q, halves[1:], state, a, b, final=True, out=out
+        )
     return out, answer
 
 

time: 103 us -> 103 us (level)
  starting transfers between devices: 28 us -> 26.8 us
    ppermute x3, waiting for transfers between devices: 0.12 us -> 1.89 us  [head_hop(): lax.ppermute(value, 'head', [(i, i ^ 1 << bit) for i in range(self.n_head)])]
    ppermute x13, waiting for transfers between devices: 28.4 us -> 26.9 us  [hop(): return lax.ppermute(value, ('blk', 'head'), pairs)]
    ppermute x13, starting transfers between devices: 26.2 us -> 25.1 us  [hop(): return lax.ppermute(value, ('blk', 'head'), pairs)]
  transfers between devices with their start and end apart: 16 -> 16, of which waited for: 9 -> 6; matrix products, arithmetic and copies ran while one was open for 5% -> 5% of each run, Pallas kernels for 34% -> 36%
where the time goes in v2:
time: 103 us
  Pallas kernels  37 us (36%)
  waiting for transfers between devices  28.8 us (28%)
  starting transfers between devices  26.8 us (26%)
  local copies, waits for them, and re-layouts  4.73 us (5%)
  between operations  2.95 us (3%)
  other arithmetic  2.34 us (2%)
    ppermute x13, waiting for transfers between devices, hop(): return lax.ppermute(value, ('blk', 'head'), pairs)  26.9 us
    ppermute x13, starting transfers between devices, hop(): return lax.ppermute(value, ('blk', 'head'), pairs)  25.1 us
    pallas_call x5, Pallas kernels, anchor_call(): pl.pallas_call(functools.partial(anchor_kernel, lo, parts, seen_at, final...  18.8 us
    pallas_call x4, Pallas kernels, own_call(): pl.pallas_call(functools.partial(own_kernel, lo), grid=(n,), in_specs=[he...  11.5 us
    pallas_call x1, Pallas kernels, query_call(): pl.pallas_call(kernel, in_specs=[pl.BlockSpec(memory_space=pltpu.SMEM)] +...  4.25 us
    dynamic_slice x3, local copies, waits for them, and re-layouts, cut(): lax.dynamic_slice(x, (first, zero), sizes, allow_negative_indices=False)  2.58 us
  transfers between devices with their start and end apart: 16, of which 6 were waited for; matrix products, arithmetic and copies ran while one was open for 5% of the time, Pallas kernels for 36%

profile of v2, /device:TPU:0, one launch (start us, length us, event | category | flops | bytes accessed | tf_op | source)
XLA Modules:
  0.0 102.6 jit_solution(4613194758438756283)
XLA Ops:
  1.6 3.0 %collective-permute-start.5 = (bf16[128,1024]{1,0:T(8,128)(2,1)S(1)}, bf16[128,1024]{1,0:T(8,128)(2,1)S(1)}, u32[]{:S(2)}, u32[]{:S(2)}) collective-permute-start(bf16[128,1024]{1,0:T(8,128)(2,1)S(1)} %dynamic-slice_bitcast_fusion), channel_id=1, source_target_pairs={{0,4},{1,9},{2,6},{3,11},{4,0},{5,13},{6,2},{7,15},{8,12},{9,1},{1... | collective-permute-start | bytes 786440 | tf_op jit(solution)/shard_map/ppermute | solution.py:58
  11.6 2.1 %collective-permute-start.6 = (bf16[128,1024]{1,0:T(8,128)(2,1)S(1)}, bf16[128,1024]{1,0:T(8,128)(2,1)S(1)}, u32[]{:S(2)}, u32[]{:S(2)}) collective-permute-start(bf16[128,1024]{1,0:T(8,128)(2,1)S(1)} %dynamic-slice_select_fusion), channel_id=1, source_target_pairs={{0,8},{1,25},{2,10},{3,27},{4,12},{5,29},{6,14},{7,31},{8,0},{9,17... | collective-permute-start | bytes 786440 | tf_op jit(solution)/shard_map/ppermute | solution.py:58
  13.7 7.2 %collective-permute-done.6 = bf16[128,1024]{1,0:T(8,128)(2,1)S(1)} collective-permute-done((bf16[128,1024]{1,0:T(8,128)(2,1)S(1)}, bf16[128,1024]{1,0:T(8,128)(2,1)S(1)}, u32[]{:S(2)}, u32[]{:S(2)}) %collective-permute-start.6) | collective-permute-done | bytes 262176 | tf_op jit(solution)/shard_map/ppermute | solution.py:58
  20.9 5.6 %collective-permute-start.7 = (bf16[128,1024]{1,0:T(8,128)(2,1)S(1)}, bf16[128,1024]{1,0:T(8,128)(2,1)S(1)}, u32[]{:S(2)}, u32[]{:S(2)}) collective-permute-start(bf16[128,1024]{1,0:T(8,128)(2,1)S(1)} %broadcast_select_fusion), channel_id=1, source_target_pairs={{0,24},{1,5},{2,26},{3,7},{4,28},{5,1},{6,30},{7,3},{8,16},{9,13},... | collective-permute-start | bytes 786440 | tf_op jit(solution)/shard_map/ppermute | solution.py:58
  26.8 6.2 %collective-permute-done.7 = bf16[128,1024]{1,0:T(8,128)(2,1)S(1)} collective-permute-done((bf16[128,1024]{1,0:T(8,128)(2,1)S(1)}, bf16[128,1024]{1,0:T(8,128)(2,1)S(1)}, u32[]{:S(2)}, u32[]{:S(2)}) %collective-permute-start.7) | collective-permute-done | bytes 262176 | tf_op jit(solution)/shard_map/ppermute | solution.py:58
  33.0 1.7 %collective-permute-start.8 = (bf16[128,1024]{1,0:T(8,128)(2,1)S(1)}, bf16[128,1024]{1,0:T(8,128)(2,1)S(1)}, u32[]{:S(2)}, u32[]{:S(2)}) collective-permute-start(bf16[128,1024]{1,0:T(8,128)(2,1)S(1)} %broadcast_select_fusion.1.refs_1_), channel_id=1, source_target_pairs={{0,4},{1,9},{2,6},{3,11},{4,0},{5,13},{6,2},{7,15},{8,12},{9,1},{1... | collective-permute-start | bytes 786440 | tf_op jit(solution)/shard_map/ppermute | solution.py:58
  34.8 3.9 %collective-permute-done.1 = bf16[256,512]{1,0:T(8,128)(2,1)S(1)} collective-permute-done((bf16[256,512]{1,0:T(8,128)(2,1)S(1)}, bf16[256,512]{1,0:T(8,128)(2,1)S(1)}, u32[]{:S(2)}, u32[]{:S(2)}) %collective-permute-start.1) | collective-permute-done | bytes 262176 | tf_op jit(solution)/shard_map/ppermute | solution.py:58
  40.3 4.2 %query.1 = (f32[128,1024]{1,0:T(8,128)S(1)}, f32[128,128]{1,0:T(8,128)S(1)}, bf16[128,1152]{1,0:T(8,128)(2,1)S(1)}) custom-call(s32[15]{0:T(128)S(1)} %stack.57.n_ref.refs_0_, bf16[128,1024]{1,0:T(8,128)(2,1)S(1)} %broadcast_select_fusion.1.refs_1_, bf16[128,1024]{1,0:T(8,128)(2,1)S(1)} %collective-permute-done.8.refs_2_, bf16[1024,256]{1,0:T(8,128)(2,1)S(1)} %copy-done.3, ...), custom_call_target="tpu_custom_call" | custom-call | flops 2415919104 | bytes 1048576 | tf_op jit(solution)/shard_map/query/pallas_call | solution.py:349
  44.5 2.2 %collective-permute-start.9 = (bf16[128,1152]{1,0:T(8,128)(2,1)S(1)}, bf16[128,1152]{1,0:T(8,128)(2,1)S(1)}, u32[]{:S(2)}, u32[]{:S(2)}) collective-permute-start(bf16[128,1152]{1,0:T(8,128)(2,1)S(1)} %get-tuple-element.67), channel_id=1, source_target_pairs={{0,4},{1,9},{2,6},{3,11},{4,0},{5,13},{6,2},{7,15},{8,12},{9,1},{1... | collective-permute-start | bytes 884744 | tf_op jit(solution)/shard_map/ppermute | solution.py:58
  46.8 2.8 %own.4 = (f32[1024,1024]{1,0:T(8,128)S(1)}, f32[1024,128]{1,0:T(8,128)S(1)}) custom-call(bf16[1024,1024]{1,0:T(8,128)(2,1)S(1)} %copy-done, bf16[1024,256]{1,0:T(8,128)(2,1)S(1)} %copy-done.3, bf16[1024,256]{1,0:T(8,128)(2,1)S(1)} %copy-done.2), custom_call_target="tpu_custom_call" | custom-call | flops 2147483648 | bytes 2621440 | tf_op jit(solution)/shard_map/own/pallas_call | solution.py:145
  49.6 2.9 %own.5 = (f32[1024,1024]{1,0:T(8,128)S(1)}, f32[1024,128]{1,0:T(8,128)S(1)}) custom-call(bf16[1024,1024]{1,0:T(8,128)(2,1)S(1)} %copy-done, bf16[1024,256]{1,0:T(8,128)(2,1)S(1)} %copy-done.3, bf16[1024,256]{1,0:T(8,128)(2,1)S(1)} %copy-done.2, f32[1024,1024]{1,0:T(8,128)S(1)} %get-tuple-element.49.refs_0_, ...), custom_call_target="tpu_custom_call", output_to_operand_aliasing={{0}: (3, {}), {1}: (4, {})} | custom-call | flops 2147483648 | bytes 2621440 | tf_op jit(solution)/shard_map/own/pallas_call | solution.py:145
  53.0 5.3 %collective-permute-start.10 = (bf16[128,1152]{1,0:T(8,128)(2,1)S(1)}, bf16[128,1152]{1,0:T(8,128)(2,1)S(1)}, u32[]{:S(2)}, u32[]{:S(2)}) collective-permute-start(bf16[128,1152]{1,0:T(8,128)(2,1)S(1)} %get-tuple-element.70), channel_id=1, source_target_pairs={{0,8},{1,25},{2,10},{3,27},{4,12},{5,29},{6,14},{7,31},{8,0},{9,17... | collective-permute-start | bytes 884744 | tf_op jit(solution)/shard_map/ppermute | solution.py:58
  58.5 2.9 %own.6 = (f32[1024,1024]{1,0:T(8,128)S(1)}, f32[1024,128]{1,0:T(8,128)S(1)}) custom-call(bf16[1024,1024]{1,0:T(8,128)(2,1)S(1)} %copy-done, bf16[1024,256]{1,0:T(8,128)(2,1)S(1)} %copy-done.3, bf16[1024,256]{1,0:T(8,128)(2,1)S(1)} %copy-done.2, f32[1024,1024]{1,0:T(8,128)S(1)} %get-tuple-element.51.refs_0_, ...), custom_call_target="tpu_custom_call", output_to_operand_aliasing={{0}: (3, {}), {1}: (4, {})} | custom-call | flops 2147483648 | bytes 2621440 | tf_op jit(solution)/shard_map/own/pallas_call | solution.py:145
  61.4 3.8 %collective-permute-done.10.got_ref = bf16[128,1152]{1,0:T(8,128)(2,1)S(1)} collective-permute-done((bf16[128,1152]{1,0:T(8,128)(2,1)S(1)}, bf16[128,1152]{1,0:T(8,128)(2,1)S(1)}, u32[]{:S(2)}, u32[]{:S(2)}) %collective-permute-start.10) | collective-permute-done | bytes 294944 | tf_op jit(solution)/shard_map/ppermute | solution.py:58
  66.8 2.9 %own.7 = (f32[1024,1024]{1,0:T(8,128)S(1)}, f32[1024,128]{1,0:T(8,128)S(1)}) custom-call(bf16[1024,1024]{1,0:T(8,128)(2,1)S(1)} %copy-done, bf16[1024,256]{1,0:T(8,128)(2,1)S(1)} %copy-done.3, bf16[1024,256]{1,0:T(8,128)(2,1)S(1)} %copy-done.2, f32[1024,1024]{1,0:T(8,128)S(1)} %get-tuple-element.53.refs_0_, ...), custom_call_target="tpu_custom_call", output_to_operand_aliasing={{0}: (3, {}), {1}: (4, {})} | custom-call | flops 2147483648 | bytes 2621440 | tf_op jit(solution)/shard_map/own/pallas_call | solution.py:145
  69.8 1.6 %collective-permute-start.4 = (bf16[512,512]{1,0:T(8,128)(2,1)S(1)}, bf16[512,512]{1,0:T(8,128)(2,1)S(1)}, u32[]{:S(2)}, u32[]{:S(2)}) collective-permute-start(bf16[512,512]{1,0:T(8,128)(2,1)S(1)} %pad_maximum_fusion.1.refs_0_.refs_1_.refs_2_.refs_3_.refs_4_.refs_5_), channel_id=1, source_target_pairs={{0,4},{1,9},{2,6},{3,11},{4,0},{5,13},{6,2},{7,15},{8,12},{9,1},{1... | collective-permute-start | bytes 1572872 | tf_op jit(solution)/shard_map/ppermute | solution.py:58
  71.4 5.9 %collective-permute-done.11.got_ref = bf16[128,1152]{1,0:T(8,128)(2,1)S(1)} collective-permute-done((bf16[128,1152]{1,0:T(8,128)(2,1)S(1)}, bf16[128,1152]{1,0:T(8,128)(2,1)S(1)}, u32[]{:S(2)}, u32[]{:S(2)}) %collective-permute-start.11) | collective-permute-done | bytes 294944 | tf_op jit(solution)/shard_map/ppermute | solution.py:58
  78.2 6.0 %anchor.5 = (f32[1024,1024]{1,0:T(8,128)S(1)}, f32[1024,128]{1,0:T(8,128)S(1)}) custom-call(s32[15]{0:T(128)S(1)} %stack.57.n_ref.refs_0_, bf16[1024,1024]{1,0:T(8,128)(2,1)S(1)} %copy-done, bf16[512,512]{1,0:T(8,128)(2,1)S(1)} %pad_maximum_fusion.1.refs_0_.refs_1_.refs_2_.refs_3_.refs_4_.refs_5_, ...), custom_call_target="tpu_custom_call", output_to_operand_aliasing={{0}: (6, {}), {1}: (7, {})} | custom-call | flops 3221225472 | bytes 5242880 | tf_op jit(solution)/shard_map/anchor/pallas_call | solution.py:258
  85.4 5.5 %anchor.6.refs_10_ = bf16[1024,1024]{1,0:T(8,128)(2,1)} custom-call(s32[15]{0:T(128)S(1)} %stack.57.n_ref.refs_0_, bf16[1024,1024]{1,0:T(8,128)(2,1)S(1)} %copy-done, bf16[512,512]{1,0:T(8,128)(2,1)S(1)} %pad_maximum_fusion.1.refs_0_.refs_1_.refs_2_.refs_3_.refs_4_.refs_5_, ...), custom_call_target="tpu_custom_call" | custom-call | flops 4831838208 | bytes 3932160 | tf_op jit(solution)/shard_map/anchor/pallas_call | solution.py:258
  90.9 2.5 %anchor.7.refs_6_ = bf16[1024,1024]{1,0:T(8,128)(2,1)} custom-call(s32[15]{0:T(128)S(1)} %stack.57.n_ref.refs_0_, bf16[1024,1024]{1,0:T(8,128)(2,1)S(1)} %copy-done, bf16[512,512]{1,0:T(8,128)(2,1)S(1)} %pad_maximum_fusion.1.refs_0_.refs_1_.refs_2_.refs_3_.refs_4_.refs_5_, ...), custom_call_target="tpu_custom_call", output_to_operand_aliasing={{}: (12, {})} | custom-call | flops 1610612736 | bytes 1310720 | tf_op jit(solution)/shard_map/anchor/pallas_call | solution.py:258
  93.5 1.6 %collective-permute-start.14 = (bf16[128,512]{1,0:T(8,128)(2,1)S(1)}, bf16[128,512]{1,0:T(8,128)(2,1)S(1)}, u32[]{:S(2)}, u32[]{:S(2)}) collective-permute-start(bf16[128,512]{1,0:T(8,128)(2,1)S(1)} %add_convert_fusion.1), channel_id=1, source_target_pairs={{0,2},{1,3},{2,0},{3,1},{4,6},{5,7},{6,4},{7,5},{8,10},{9,11},{10,... | collective-permute-start | bytes 393224 | tf_op jit(solution)/shard_map/ppermute | solution.py:61
  95.1 2.5 %anchor.8.refs_6_ = bf16[1024,1024]{1,0:T(8,128)(2,1)} custom-call(s32[15]{0:T(128)S(1)} %stack.57.n_ref.refs_0_, bf16[1024,1024]{1,0:T(8,128)(2,1)S(1)} %copy-done, bf16[512,512]{1,0:T(8,128)(2,1)S(1)} %collective-permute-done.4.refs_2_.refs_3_.refs_6_.refs_7_.refs_0_.refs_1_, ...), custom_call_target="tpu_custom_call", output_to_operand_aliasing={{}: (8, {})} | custom-call | flops 1610612736 | bytes 2621440 | tf_op jit(solution)/shard_map/anchor/pallas_call | solution.py:258
  97.6 1.9 %collective-permute-done.14 = bf16[128,512]{1,0:T(8,128)(2,1)S(1)} collective-permute-done((bf16[128,512]{1,0:T(8,128)(2,1)S(1)}, bf16[128,512]{1,0:T(8,128)(2,1)S(1)}, u32[]{:S(2)}, u32[]{:S(2)}) %collective-permute-start.14) | collective-permute-done | bytes 131104 | tf_op jit(solution)/shard_map/ppermute | solution.py:61
  99.6 2.2 %anchor.9 = bf16[1024,1024]{1,0:T(8,128)(2,1)} custom-call(s32[15]{0:T(128)S(1)} %stack.57.n_ref.refs_0_, bf16[1024,1024]{1,0:T(8,128)(2,1)S(1)} %copy-done, bf16[512,512]{1,0:T(8,128)(2,1)S(1)} %collective-permute-done.4.refs_2_.refs_3_.refs_6_.refs_7_.refs_0_.refs_1_, ...), custom_call_target="tpu_custom_call", output_to_operand_aliasing={{}: (8, {})} | custom-call | flops 1610612736 | bytes 2621440 | tf_op jit(solution)/shard_map/anchor/pallas_call | solution.py:258
  (51 shorter events, 13.0 us)
Async XLA Ops:
  1.6 8.9 %collective-permute-start.5 = (bf16[128,1024]{1,0:T(8,128)(2,1)S(1)}, bf16[128,1024]{1,0:T(8,128)(2,1)S(1)}, u32[]{:S(2)}, u32[]{:S(2)}) collective-permute-start(bf16[128,1024]{1,0:T(8,128)(2,1)S(1)} %dynamic-slice_bitcast_fusion), channel_id=1, source_target_pairs={{0,4},{1,9},{2,6},{3,11},{4,0},{5,13},{6,2},{7,15},{8,12},{9,1},{1... | collective-permute-start | bytes 786440 | tf_op jit(solution)/shard_map/ppermute | solution.py:58
  8.8 31.4 %copy-start.2 = (bf16[1024,256]{1,0:T(8,128)(2,1)S(1)}, bf16[1024,256]{1,0:T(8,128)(2,1)}, u32[]{:S(2)}) copy-start(bf16[1024,256]{1,0:T(8,128)(2,1)} %refs_4_) | copy-start | bytes 1572868
  8.8 31.4 %copy-start.3 = (bf16[1024,256]{1,0:T(8,128)(2,1)S(1)}, bf16[1024,256]{1,0:T(8,128)(2,1)}, u32[]{:S(2)}) copy-start(bf16[1024,256]{1,0:T(8,128)(2,1)} %refs_3_) | copy-start | bytes 1572868
  8.8 31.4 %copy-start.4 = (bf16[1,256,256]{2,1,0:T(8,128)(2,1)S(1)}, bf16[1,256,256]{2,1,0:T(8,128)(2,1)}, u32[]{:S(2)}) copy-start(bf16[1,256,256]{2,1,0:T(8,128)(2,1)} %refs_5_.1) | copy-start | bytes 393220
  8.8 31.4 %copy-start.5 = (bf16[1,256,256]{2,1,0:T(8,128)(2,1)S(1)}, bf16[1,256,256]{2,1,0:T(8,128)(2,1)}, u32[]{:S(2)}) copy-start(bf16[1,256,256]{2,1,0:T(8,128)(2,1)} %refs_6_.1) | copy-start | bytes 393220
  10.4 16.1 %collective-permute-start = (bf16[512,512]{1,0:T(8,128)(2,1)S(1)}, bf16[512,512]{1,0:T(8,128)(2,1)S(1)}, u32[]{:S(2)}, u32[]{:S(2)}) collective-permute-start(bf16[512,512]{1,0:T(8,128)(2,1)S(1)} %pad_maximum_fusion), channel_id=1, source_target_pairs={{0,4},{1,9},{2,6},{3,11},{4,0},{5,13},{6,2},{7,15},{8,12},{9,1},{1... | collective-permute-start | bytes 1572872 | tf_op jit(solution)/shard_map/ppermute | solution.py:58
  11.6 9.3 %collective-permute-start.6 = (bf16[128,1024]{1,0:T(8,128)(2,1)S(1)}, bf16[128,1024]{1,0:T(8,128)(2,1)S(1)}, u32[]{:S(2)}, u32[]{:S(2)}) collective-permute-start(bf16[128,1024]{1,0:T(8,128)(2,1)S(1)} %dynamic-slice_select_fusion), channel_id=1, source_target_pairs={{0,8},{1,25},{2,10},{3,27},{4,12},{5,29},{6,14},{7,31},{8,0},{9,17... | collective-permute-start | bytes 786440 | tf_op jit(solution)/shard_map/ppermute | solution.py:58
  20.9 12.1 %collective-permute-start.7 = (bf16[128,1024]{1,0:T(8,128)(2,1)S(1)}, bf16[128,1024]{1,0:T(8,128)(2,1)S(1)}, u32[]{:S(2)}, u32[]{:S(2)}) collective-permute-start(bf16[128,1024]{1,0:T(8,128)(2,1)S(1)} %broadcast_select_fusion), channel_id=1, source_target_pairs={{0,24},{1,5},{2,26},{3,7},{4,28},{5,1},{6,30},{7,3},{8,16},{9,13},... | collective-permute-start | bytes 786440 | tf_op jit(solution)/shard_map/ppermute | solution.py:58
  26.7 11.9 %collective-permute-start.1 = (bf16[256,512]{1,0:T(8,128)(2,1)S(1)}, bf16[256,512]{1,0:T(8,128)(2,1)S(1)}, u32[]{:S(2)}, u32[]{:S(2)}) collective-permute-start(bf16[256,512]{1,0:T(8,128)(2,1)S(1)} %constant_dynamic-slice_fusion), channel_id=1, source_target_pairs={{0,8},{1,25},{2,10},{3,27},{4,12},{5,29},{6,14},{7,31},{8,0},{9,17... | collective-permute-start | bytes 786440 | tf_op jit(solution)/shard_map/ppermute | solution.py:58
  33.0 7.2 %collective-permute-start.8 = (bf16[128,1024]{1,0:T(8,128)(2,1)S(1)}, bf16[128,1024]{1,0:T(8,128)(2,1)S(1)}, u32[]{:S(2)}, u32[]{:S(2)}) collective-permute-start(bf16[128,1024]{1,0:T(8,128)(2,1)S(1)} %broadcast_select_fusion.1.refs_1_), channel_id=1, source_target_pairs={{0,4},{1,9},{2,6},{3,11},{4,0},{5,13},{6,2},{7,15},{8,12},{9,1},{1... | collective-permute-start | bytes 786440 | tf_op jit(solution)/shard_map/ppermute | solution.py:58
  38.7 8.0 %copy-start = (bf16[1024,1024]{1,0:T(8,128)(2,1)S(1)}, bf16[1024,1024]{1,0:T(8,128)(2,1)}, u32[]{:S(2)}) copy-start(bf16[1024,1024]{1,0:T(8,128)(2,1)} %q_ref.8) | copy-start | bytes 6291460
  38.7 19.6 %collective-permute-start.2 = (bf16[256,512]{1,0:T(8,128)(2,1)S(1)}, bf16[256,512]{1,0:T(8,128)(2,1)S(1)}, u32[]{:S(2)}, u32[]{:S(2)}) collective-permute-start(bf16[256,512]{1,0:T(8,128)(2,1)S(1)} %dynamic-slice_select_fusion.1), channel_id=1, source_target_pairs={{0,24},{1,5},{2,26},{3,7},{4,28},{5,1},{6,30},{7,3},{8,16},{9,13},... | collective-permute-start | bytes 786440 | tf_op jit(solution)/shard_map/ppermute | solution.py:58
  44.5 8.0 %collective-permute-start.9 = (bf16[128,1152]{1,0:T(8,128)(2,1)S(1)}, bf16[128,1152]{1,0:T(8,128)(2,1)S(1)}, u32[]{:S(2)}, u32[]{:S(2)}) collective-permute-start(bf16[128,1152]{1,0:T(8,128)(2,1)S(1)} %get-tuple-element.67), channel_id=1, source_target_pairs={{0,4},{1,9},{2,6},{3,11},{4,0},{5,13},{6,2},{7,15},{8,12},{9,1},{1... | collective-permute-start | bytes 884744 | tf_op jit(solution)/shard_map/ppermute | solution.py:58
  53.0 12.2 %collective-permute-start.10 = (bf16[128,1152]{1,0:T(8,128)(2,1)S(1)}, bf16[128,1152]{1,0:T(8,128)(2,1)S(1)}, u32[]{:S(2)}, u32[]{:S(2)}) collective-permute-start(bf16[128,1152]{1,0:T(8,128)(2,1)S(1)} %get-tuple-element.70), channel_id=1, source_target_pairs={{0,8},{1,25},{2,10},{3,27},{4,12},{5,29},{6,14},{7,31},{8,0},{9,17... | collective-permute-start | bytes 884744 | tf_op jit(solution)/shard_map/ppermute | solution.py:58
  58.4 11.3 %collective-permute-start.3 = (bf16[256,512]{1,0:T(8,128)(2,1)S(1)}, bf16[256,512]{1,0:T(8,128)(2,1)S(1)}, u32[]{:S(2)}, u32[]{:S(2)}) collective-permute-start(bf16[256,512]{1,0:T(8,128)(2,1)S(1)} %broadcast_select_fusion.2), channel_id=1, source_target_pairs={{0,8},{1,25},{2,10},{3,27},{4,12},{5,29},{6,14},{7,31},{8,0},{9,17... | collective-permute-start | bytes 786440 | tf_op jit(solution)/shard_map/ppermute | solution.py:58
  65.7 11.5 %collective-permute-start.11 = (bf16[128,1152]{1,0:T(8,128)(2,1)S(1)}, bf16[128,1152]{1,0:T(8,128)(2,1)S(1)}, u32[]{:S(2)}, u32[]{:S(2)}) collective-permute-start(bf16[128,1152]{1,0:T(8,128)(2,1)S(1)} %get-tuple-element.73), channel_id=1, source_target_pairs={{0,24},{1,5},{2,26},{3,7},{4,28},{5,1},{6,30},{7,3},{8,16},{9,13},... | collective-permute-start | bytes 884744 | tf_op jit(solution)/shard_map/ppermute | solution.py:58
  69.8 15.6 %collective-permute-start.4 = (bf16[512,512]{1,0:T(8,128)(2,1)S(1)}, bf16[512,512]{1,0:T(8,128)(2,1)S(1)}, u32[]{:S(2)}, u32[]{:S(2)}) collective-permute-start(bf16[512,512]{1,0:T(8,128)(2,1)S(1)} %pad_maximum_fusion.1.refs_0_.refs_1_.refs_2_.refs_3_.refs_4_.refs_5_), channel_id=1, source_target_pairs={{0,4},{1,9},{2,6},{3,11},{4,0},{5,13},{6,2},{7,15},{8,12},{9,1},{1... | collective-permute-start | bytes 1572872 | tf_op jit(solution)/shard_map/ppermute | solution.py:58
  77.7 6.6 %collective-permute-start.12 = (bf16[128,1024]{1,0:T(8,128)(2,1)S(1)}, bf16[128,1024]{1,0:T(8,128)(2,1)S(1)}, u32[]{:S(2)}, u32[]{:S(2)}) collective-permute-start(bf16[128,1024]{1,0:T(8,128)(2,1)S(1)} %merge.5.mine_ref), channel_id=1, source_target_pairs={{0,4},{1,9},{2,6},{3,11},{4,0},{5,13},{6,2},{7,15},{8,12},{9,1},{1... | collective-permute-start | bytes 786440 | tf_op jit(solution)/shard_map/ppermute | solution.py:58
  78.2 6.0 %copy-start.1 = (bf16[1024,512]{1,0:T(8,128)(2,1)S(1)}, bf16[1024,512]{1,0:T(8,128)(2,1)}, u32[]{:S(2)}) copy-start(bf16[1024,512]{1,0:T(8,128)(2,1)} %w_ref.1) | copy-start | bytes 3145732
  85.3 8.1 %collective-permute-start.13 = (f32[128,512]{1,0:T(8,128)S(1)}, f32[128,512]{1,0:T(8,128)S(1)}, u32[]{:S(2)}, u32[]{:S(2)}) collective-permute-start(f32[128,512]{1,0:T(8,128)S(1)} %slice_select_fusion), channel_id=1, source_target_pairs={{0,1},{1,0},{2,3},{3,2},{4,5},{5,4},{6,7},{7,6},{8,9},{9,8},{10,11... | collective-permute-start | bytes 786440 | tf_op jit(solution)/shard_map/ppermute | solution.py:61
  93.5 6.0 %collective-permute-start.14 = (bf16[128,512]{1,0:T(8,128)(2,1)S(1)}, bf16[128,512]{1,0:T(8,128)(2,1)S(1)}, u32[]{:S(2)}, u32[]{:S(2)}) collective-permute-start(bf16[128,512]{1,0:T(8,128)(2,1)S(1)} %add_convert_fusion.1), channel_id=1, source_target_pairs={{0,2},{1,3},{2,0},{3,1},{4,6},{5,7},{6,4},{7,5},{8,10},{9,11},{10,... | collective-permute-start | bytes 393224 | tf_op jit(solution)/shard_map/ppermute | solution.py:61
  99.5 2.3 %collective-permute-start.15 = (bf16[128,512]{1,0:T(8,128)(2,1)S(1)}, bf16[128,512]{1,0:T(8,128)(2,1)S(1)}, u32[]{:S(2)}, u32[]{:S(2)}) collective-permute-start(bf16[128,512]{1,0:T(8,128)(2,1)S(1)} %add_convert_fusion), channel_id=1, source_target_pairs={{0,1},{1,0},{2,3},{3,2},{4,5},{5,4},{6,7},{7,6},{8,9},{9,8},{10,11... | collective-permute-start | bytes 393224 | tf_op jit(solution)/shard_map/ppermute | solution.py:61
